TPU v7x, 128 devices: a whole 4x4x4 slice. The times are simulated.
128 devices in a mesh: inst: 4 (over x_lo, core), space: 32 (over y, x_hi, z).
Axes of the slice: x: 4 (x_hi: 2, x_lo: 2; x = x_hi * 2 + x_lo), y: 4, z: 4, core: 2. Of those that a mesh axis runs over, the one named last changes fastest.
Arguments:
- adjoint_old: float32 [8, 6, 2048, 512], P('inst', None, 'space'), may hold values from -6 to 6
- source_term: float32 [8, 6, 2048, 512], P('inst', None, 'space'), may hold values from -6 to 6
- face_stream: float32 [8, 2048, 512], P('inst', 'space'), may hold values from 0.2 to 1
- face_pitch: float32 [8, 2048, 512], P('inst', 'space'), may hold values from 0.2 to 1
- diag_scale: float32 [8, 2048, 512], P('inst', 'space'), may hold values from 0.1 to 0.4
- volume: float32 [2048, 512], P('space'), may hold values from 0.5 to 2
- face_blocks: float32 [4, 6, 6], replicated, may hold values from -2.5 to 2.5
- diag_inverse: float32 [8, 6, 6], P('inst')
- periodic_block: float32 [6, 6], replicated, may hold values from -2.5 to 2.5
- frequency: float32 [1], replicated, may hold values from 0.5 to 2
- phase_shift: int32 [1], replicated, may hold values from 1 to 7
- periodic_cells: int32 [32, 32, 128], P('space'), may hold values from 0 to 32767
- periodic_targets: int32 [32, 32, 128], P(None, 'space'), may hold values from 0 to 32767
- periodic_weights: float32 [32, 32, 128], P('space'), may hold values from 0.5 to 1.5
- periodic_counts: int32 [32, 32], P('space'), may hold values from 0 to 128, as said below
Outputs:
- adjoint_new: float32 [8, 6, 2048, 512], P('inst', None, 'space')
- residual: float32 [8, 6, 2048, 512], P('inst', None, 'space')
Inputs may be any that keep to these rules, and one draw needn't show every extreme that they name: `periodic_counts`: each partition's row has one peer with 128 live faces, and one partition receives 128 live faces from every partition. `periodic_cells`: local cell indices in the sending partition. `periodic_targets`: local cell indices in the receiving partition.
All inputs are finite; a program needn't handle non-finite values.
Results may differ from a plain program's by a relative error of at most 0.0001.
Values sent between devices are 32-bit elements; how exact they have to be, the bound alone decides.
No kernel may reach another device: no remote copies, remote signals or barrier semaphores. Data moves between devices by JAX's collectives and lax.ppermute only.
A program may use at most 128 MiB of HBM per device.

v0:
```python
import math

import jax
import jax.numpy as jnp
import numpy as np
from jax import lax
from jax.experimental import pallas as pl
from jax.experimental.pallas import tpu as pltpu
from jax.sharding import PartitionSpec as P

INSTANCES = 8
BLK = 8
SEND = ((0, 2), (2, 6))
PIECES = ((0, 2), (2, 2), (4, 2), (6, 2))
VMEM = 48 * 1024 * 1024
HIGH = lax.Precision.HIGHEST


def coef(k):
    k = k % INSTANCES
    if k in (0, 4):
        return 0.0
    return 0.5 * (-1.0) ** k / math.tan(math.pi * k / INSTANCES)


def partner(value, bit):
    return lax.ppermute(value, "inst", [(i, i ^ bit) for i in range(4)])


def from_behind(value, steps):
    count = lax.axis_size("space")
    first, last = max(0, -steps), min(count, count - steps)
    return lax.ppermute(value, "space", [(s, s + steps) for s in range(first, last)])


def smem():
    return pl.BlockSpec(memory_space=pltpu.SMEM)


def params():
    return pltpu.CompilerParams(vmem_limit_bytes=VMEM)


def split(x):
    hi = x.astype(jnp.bfloat16)
    lo = (x - hi.astype(jnp.float32)).astype(jnp.bfloat16)
    return hi, lo


def pick_kernel(pb_ref, cnt_ref, a_ref, fs_ref, cell_ref, wt_ref, out_ref, lo_ref, hi_ref, tab):
    step = pl.program_id(0)

    @pl.when(step == 0)
    def _():
        for f in range(12):
            hi, lo = split(a_ref[f])
            tab[f * 64 : f * 64 + 64, 0:512] = hi
            tab[f * 64 : f * 64 + 64, 512:1024] = lo
        for f in range(12):
            lo_ref[f : f + 1, :] = fs_ref[f // 6, 7:8, :] * a_ref[f, 63:64, :]
            hi_ref[f : f + 1, :] = a_ref[f, 0:1, :]

    cells = cell_ref[...]
    cols = lax.bitwise_and(cells, 511)
    rows = lax.shift_right_logical(cells, 9)
    lane = lax.broadcasted_iota(jnp.int32, (512, 128), 0)
    sub = lax.broadcasted_iota(jnp.int32, (64, 128), 0)
    slot = lax.broadcasted_iota(jnp.int32, (1, 128), 1)
    for half in range(2):
        hot = jnp.concatenate(
            [
                jnp.where(lane == cols[q : q + 1, :], 1.0, 0.0).astype(jnp.bfloat16)
                for q in range(4 * half, 4 * half + 4)
            ],
            axis=1,
        )
        part = jnp.dot(tab[...], jnp.concatenate([hot, hot], axis=0), preferred_element_type=jnp.float32)
        for k in range(4):
            q = 4 * half + k
            mask = sub == rows[q : q + 1, :]
            weight = jnp.where(slot < cnt_ref[0, step * 8 + q], wt_ref[q : q + 1, :], 0.0)
            for g in range(2):
                got = []
                for v in range(6):
                    f = g * 6 + v
                    mine = part[f * 64 : f * 64 + 64, k * 128 : k * 128 + 128]
                    got.append(jnp.sum(jnp.where(mask, mine, 0.0), axis=0, keepdims=True))
                for u in range(6):
                    total = pb_ref[0, u] * got[0]
                    for v in range(1, 6):
                        total = total + pb_ref[v, u] * got[v]
                    out_ref[g, u, q : q + 1, :] = total * weight


def pick(block, counts, a, fs, cells, weights):
    return pl.pallas_call(
        pick_kernel,
        name="pick",
        grid=(4,),
        in_specs=[
            smem(),
            smem(),
            pl.BlockSpec((12, 64, 512), lambda i: (0, 0, 0)),
            pl.BlockSpec((2, 8, 512), lambda i: (0, 7, 0)),
            pl.BlockSpec((8, 128), lambda i: (i, 0)),
            pl.BlockSpec((8, 128), lambda i: (i, 0)),
        ],
        out_specs=[
            pl.BlockSpec((2, 6, 8, 128), lambda i: (0, 0, i, 0)),
            pl.BlockSpec((12, 512), lambda i: (0, 0)),
            pl.BlockSpec((12, 512), lambda i: (0, 0)),
        ],
        out_shape=[
            jax.ShapeDtypeStruct((2, 6, 32, 128), jnp.float32),
            jax.ShapeDtypeStruct((12, 512), jnp.float32),
            jax.ShapeDtypeStruct((12, 512), jnp.float32),
        ],
        scratch_shapes=[pltpu.VMEM((768, 1024), jnp.bfloat16)],
        compiler_params=params(),
    )(block, counts, a, fs, cells, weights)


def place_kernel(row0, rows_here, val_ref, tgt_ref, out_ref):
    step = pl.program_id(0)
    cells = tgt_ref[...]
    cols = lax.bitwise_and(cells, 511)
    rows = lax.shift_right_logical(cells, 9) - row0
    lane = lax.broadcasted_iota(jnp.int32, (512, 128), 0)
    sub = lax.broadcasted_iota(jnp.int32, (rows_here, 128), 0)
    hot = jnp.concatenate(
        [jnp.where(lane == cols[p : p + 1, :], 1.0, 0.0).astype(jnp.bfloat16) for p in range(8)], axis=1
    )
    highs, lows = [], []
    for p in range(8):
        mask = sub == rows[p : p + 1, :]
        spread = [jnp.where(mask, val_ref[p, f : f + 1, :], 0.0) for f in range(12)]
        hi, lo = split(jnp.concatenate(spread, axis=0))
        highs.append(hi)
        lows.append(lo)
    dims = (((1,), (1,)), ((), ()))
    total = lax.dot_general(
        jnp.concatenate(highs + lows, axis=1),
        jnp.concatenate([hot, hot], axis=1),
        dims,
        preferred_element_type=jnp.float32,
    )
    total = total.reshape(12, rows_here, 512)

    @pl.when(step == 0)
    def _():
        out_ref[...] = total

    @pl.when(step > 0)
    def _():
        out_ref[...] += total


def place(values, targets, piece):
    b0, nb = piece
    rows = nb * BLK

    def kernel(*refs):
        place_kernel(b0 * BLK, rows, *refs)

    return pl.pallas_call(
        kernel,
        name="place",
        grid=(4,),
        in_specs=[
            pl.BlockSpec((8, 12, 128), lambda i: (i, 0, 0)),
            pl.BlockSpec((8, 128), lambda i: (i, 0)),
        ],
        out_specs=pl.BlockSpec((12, rows, 512), lambda i: (0, 0, 0)),
        out_shape=jax.ShapeDtypeStruct((12, rows, 512), jnp.float32),
        compiler_params=params(),
    )(values, targets)


def own_terms(core, j):
    own = [coef(i - j) for i in range(2)]
    sib = [(coef(2 + i - j), coef(-2 + i - j)) for i in range(2)]
    return own, [jnp.where(core == 0, jnp.float32(e), jnp.float32(o)) for e, o in sib]


def far_terms(core, j):
    par = [coef(4 + i - j) for i in range(2)]
    sp = [(coef(6 + i - j), coef(2 + i - j)) for i in range(2)]
    return par, [jnp.where(core == 0, jnp.float32(e), jnp.float32(o)) for e, o in sp]


def weighted(terms, fields):
    total = None
    for c, x in zip(terms, fields):
        if isinstance(c, float) and c == 0.0:
            continue
        total = c * x if total is None else total + c * x
    return total


def sweep_kernel(
    last_sweep, b0, nb, fb_ref, di_ref, fr_ref, cur, prev, nxt, hlo, hhi, src, fs_ref, fsp_ref, fp_ref, dg_ref,
    vol_ref, per_ref, sib, *rest,
):
    step = pl.program_id(0)
    blk = b0 + step
    core = lax.rem(lax.axis_index("inst"), 2)
    if last_sweep:
        (far,), rest = rest[:1], rest[1:]
        out, res_out = rest[-2:]
    else:
        (par, sp), rest = rest[:2], rest[2:]
        out, piece, edge_lo, edge_hi = rest[-4:]
    row = lax.broadcasted_iota(jnp.int32, (BLK, 512), 0)
    col = lax.broadcasted_iota(jnp.int32, (BLK, 512), 1)
    top, bottom = row == 0, row == BLK - 1
    left, right = col == 0, col == 511
    fv = fr_ref[0] * vol_ref[...]
    for g in range(2):
        fs, fp, dg = fs_ref[g], fp_ref[g], dg_ref[g]
        fs_before = fsp_ref[g, BLK - 1 : BLK, :]
        own_w, sib_w = own_terms(core, g)
        if not last_sweep:
            par_w, sp_w = far_terms(core, g)
        r = [src[g, u] - per_ref[g * 6 + u] for u in range(6)]
        for v in range(6):
            f = g * 6 + v
            a = cur[g, v]
            before = jnp.where(blk == 0, hlo[f : f + 1, :], fs_before * prev[g, v, BLK - 1 : BLK, :])
            after = jnp.where(blk == 7, hhi[f : f + 1, :], nxt[g, v, 0:1, :])
            lower = jnp.where(top, before, pltpu.roll(fs * a, 1, 0))
            upper = fs * jnp.where(bottom, after, pltpu.roll(a, BLK - 1, 0))
            lft = jnp.where(left, 0.0, pltpu.roll(fp * a, 1, 1))
            rgt = fp * jnp.where(right, 0.0, pltpu.roll(a, 511, 1))
            for u in range(6):
                r[u] = r[u] - (
                    (fb_ref[0, v, u] * lower + fb_ref[1, v, u] * upper)
                    + (fb_ref[2, v, u] * lft + fb_ref[3, v, u] * rgt)
                )
            mixed = weighted(own_w + sib_w, [cur[0, v], cur[1, v], sib[0, v], sib[1, v]])
            if last_sweep:
                mixed = mixed + far[g, v]
            else:
                mixed = mixed + weighted(par_w + sp_w, [par[0, v], par[1, v], sp[0, v], sp[1, v]])
            r[v] = r[v] - fv * mixed
        for u in range(6):
            total = di_ref[g, u, 0] * r[0]
            for v in range(1, 6):
                total = total + di_ref[g, u, v] * r[v]
            new = dg * total
            out[g, u] = new
            if last_sweep:
                res_out[g, u] = r[u]
            else:
                piece[g, u] = new
                f = g * 6 + u

                @pl.when(blk == 7)
                def _(new=new, f=f, fs=fs):
                    edge_lo[f : f + 1, :] = (fs * new)[BLK - 1 : BLK, :]

                @pl.when(blk == 0)
                def _(new=new, f=f):
                    edge_hi[f : f + 1, :] = new[0:1, :]


def sweep(last_sweep, piece, common, a, halo, per, sib, sib_b0, far, far_b0, into):
    b0, nb = piece
    fb, di, fr, src, fs, fp, dg, vol = common
    big = (2, 6, BLK, 512)
    small = (2, BLK, 512)

    def at(off):
        return lambda i: (0, 0, off + i, 0)

    def at3(off):
        return lambda i: (0, off + i, 0)

    halo_spec = pl.BlockSpec((12, 512), lambda i: (0, 0))
    specs = [
        smem(), smem(), smem(),
        pl.BlockSpec(big, at(b0)),
        pl.BlockSpec(big, lambda i: (0, 0, jnp.maximum(b0 + i - 1, 0), 0)),
        pl.BlockSpec(big, lambda i: (0, 0, jnp.minimum(b0 + i + 1, 7), 0)),
        halo_spec, halo_spec,
        pl.BlockSpec(big, at(b0)),
        pl.BlockSpec(small, at3(b0)),
        pl.BlockSpec(small, lambda i: (0, jnp.maximum(b0 + i - 1, 0), 0)),
        pl.BlockSpec(small, at3(b0)),
        pl.BlockSpec(small, at3(b0)),
        pl.BlockSpec((BLK, 512), lambda i: (b0 + i, 0)),
        pl.BlockSpec((12, BLK, 512), at3(0)),
        pl.BlockSpec(big, at(sib_b0)),
    ]
    args = [fb, di, fr, a, a, a, halo[0], halo[1], src, fs, fs, fp, dg, vol, per, sib]
    for x in far:
        specs.append(pl.BlockSpec(big, at(far_b0)))
        args.append(x)
    full = jax.ShapeDtypeStruct((2, 6, 64, 512), jnp.float32)
    out_specs = [pl.BlockSpec(big, at(b0))]
    out_shape = [full]
    if last_sweep:
        out_specs.append(pl.BlockSpec(big, at(b0)))
        out_shape.append(full)
    else:
        out_specs += [pl.BlockSpec(big, at(0)), halo_spec, halo_spec]
        out_shape += [
            jax.ShapeDtypeStruct((2, 6, nb * BLK, 512), jnp.float32),
            jax.ShapeDtypeStruct((12, 512), jnp.float32),
            jax.ShapeDtypeStruct((12, 512), jnp.float32),
        ]
    aliases = {}
    if into is not None:
        for k, x in enumerate(into):
            aliases[len(args)] = k
            specs.append(pl.BlockSpec(memory_space=pl.ANY))
            args.append(x)

    def kernel(*refs):
        sweep_kernel(last_sweep, b0, nb, *refs)

    return pl.pallas_call(
        kernel,
        name="sweep2" if last_sweep else "sweep1",
        grid=(nb,),
        in_specs=specs,
        out_specs=out_specs,
        out_shape=out_shape,
        input_output_aliases=aliases,
        compiler_params=params(),
    )(*args)


def combine_kernel(own, sib, out):
    core = lax.rem(lax.axis_index("inst"), 2)
    for j in range(2):
        own_w, sib_w = far_terms(core, j)
        for v in range(6):
            out[j, v] = weighted(own_w + sib_w, [own[0, v], own[1, v], sib[0, v], sib[1, v]])


def combine(own, sib):
    big = (2, 6, BLK, 512)
    spec = pl.BlockSpec(big, lambda i: (0, 0, i, 0))
    return pl.pallas_call(
        combine_kernel,
        name="combine",
        grid=(own.shape[2] // BLK,),
        in_specs=[spec, spec],
        out_specs=spec,
        out_shape=jax.ShapeDtypeStruct(own.shape, jnp.float32),
        compiler_params=params(),
    )(own, sib)


def body(
    adjoint_old, source_term, face_stream, face_pitch, diag_scale, volume, face_blocks, diag_inverse,
    periodic_block, frequency, phase_shift, periodic_cells, periodic_targets, periodic_weights, periodic_counts,
):
    position = lax.axis_index("inst")
    common = (face_blocks, diag_inverse, frequency, source_term, face_stream, face_pitch, diag_scale, volume)

    parts = [adjoint_old[:, :, b * BLK : (b + n) * BLK] for b, n in SEND]
    first = partner(parts[0], 2)
    out, lo, hi = pick(
        periodic_block, periodic_counts, adjoint_old.reshape(12, 64, 512), face_stream, periodic_cells[0],
        periodic_weights[0],
    )
    out_par = partner(out, 2)
    out_sib = partner(out, 1)
    later = [partner(x, 2) for x in parts[1:]]
    sib0 = partner(adjoint_old, 1)
    halo0 = (from_behind(lo, 1), from_behind(hi, -1))
    out_sp = partner(out_par, 1)

    pool = [(out, position), (out_sib, position ^ 1), (out_par, position ^ 2), (out_sp, position ^ 3)]
    chosen = []
    for j in range(2):
        want = lax.rem(2 * position + j - phase_shift[0] + INSTANCES, INSTANCES)
        value = jnp.zeros((6, 32, 128), jnp.float32)
        for x, home in pool:
            for i in range(2):
                value = jnp.where(want == 2 * home + i, x[i], value)
        chosen.append(value)
    routed = jnp.concatenate(chosen, axis=0).transpose(1, 0, 2)
    arrived = lax.all_to_all(routed, "space", split_axis=0, concat_axis=0, tiled=True)
    targets = periodic_targets[:, 0, :]

    par0 = [first] + later
    sp0 = [partner(x, 1) for x in par0]

    a1, pieces, pers = None, [], []
    edge_lo = edge_hi = None
    for b0, nb in PIECES:
        per = place(arrived, targets, (b0, nb))
        which = [k for k, (s, n) in enumerate(SEND) if s <= b0 and b0 + nb <= s + n][0]
        a1, piece, e_lo, e_hi = sweep(
            False, (b0, nb), common, adjoint_old, halo0, per, sib0, b0, (par0[which], sp0[which]),
            b0 - SEND[which][0], None if a1 is None else (a1,),
        )
        if b0 == 0:
            edge_hi = e_hi
        if b0 + nb == 8:
            edge_lo = e_lo
        sib1 = partner(piece, 1)
        far = partner(combine(piece, sib1), 2)
        pieces.append((b0, nb, sib1, far))
        pers.append(per)
    halo1 = (from_behind(edge_lo, 1), from_behind(edge_hi, -1))
    outs = None
    for (b0, nb, sib1, far), per in zip(pieces, pers):
        outs = sweep(True, (b0, nb), common, a1, halo1, per, sib1, 0, (far,), 0, outs)
    return (outs[0], outs[1])


def solution(mesh):
    in_specs = (
        P("inst", None, "space", None),
        P("inst", None, "space", None),
        P("inst", "space", None),
        P("inst", "space", None),
        P("inst", "space", None),
        P("space", None),
        P(),
        P("inst", None, None),
        P(),
        P(),
        P(),
        P("space", None, None),
        P(None, "space", None),
        P("space", None, None),
        P("space", None),
    )
    out_specs = (P("inst", None, "space", None), P("inst", None, "space", None))
    return jax.shard_map(body, mesh=mesh, in_specs=in_specs, out_specs=out_specs, check_vma=False)
```

profile of v0, /device:TPU:8, one launch (start us, length us, event | category | flops | bytes accessed | tf_op | source)
XLA Modules:
  0.0 166.8 jit_solution(9043031844216632204)
XLA Ops:
  0.7 1.5 slice.46
  2.2 1.6 collective-permute-start.6
  3.8 0.8 slice.47
  4.5 0.5 collective-permute-start.8
  5.1 9.3 %pick.1 = (f32[2,6,32,128]{3,2,1,0:T(8,128)S(1)}, f32[12,512]{1,0:T(8,128)S(1)}, f32[12,512]{1,0:T(8,128)S(1)}) custom-call(f32[6,6]{1,0:T(8,128)S(1)} %copy-done.10, s32[1,32]{1,0:T(1,128)S(1)} %copy-done.11, f32[12,64,512]{2,1,0:T(8,128)S(1)} %bitcast.13, f32[2,64,512]{2,1,0:T(8,128)S(1)} %copy-done.2, s32[32,128]{1,0:T(8,128)S(1)} %bitcast.18, ...), custom_call_target="tpu_custom_call" | custom-call | tf_op jit(solution)/shard_map/pick/pallas_call | solution.py:96
  14.4 0.1 copy.26
  14.5 1.6 collective-permute-start.2
  16.1 15.0 %collective-permute-done.6.refs_16_ = f32[2,6,48,512]{3,2,1,0:T(8,128)S(1)} collective-permute-done((f32[2,6,48,512]{3,2,1,0:T(8,128)S(1)}, f32[2,6,48,512]{3,2,1,0:T(8,128)S(1)}, u32[]{:S(2)}, u32[]{:S(2)}) %collective-permute-start.6) | collective-permute-done | bytes 1179680 | tf_op jit(solution)/shard_map/ppermute | solution.py:27
  31.1 0.5 collective-permute-start.4
  31.6 12.4 %collective-permute-done.2 = f32[2,6,32,128]{3,1,2,0:T(8,128)S(1)} collective-permute-done((f32[2,6,32,128]{3,1,2,0:T(8,128)S(1)}, f32[2,6,32,128]{3,1,2,0:T(8,128)S(1)}, u32[]{:S(2)}, u32[]{:S(2)}) %collective-permute-start.2) | collective-permute-done | bytes 196640 | tf_op jit(solution)/shard_map/ppermute | solution.py:27
  44.7 0.6 collective-permute-start.9
  45.3 0.4 collective-permute-done.3
  45.7 1.2 select_bitcast_fusion.1
  46.8 1.2 select_bitcast_fusion
  48.0 0.7 maximum_bitcast_fusion
  48.7 11.2 %all-to-all-start = ((f32[32,12,128]{2,1,0:T(8,128)}), f32[32,12,128]{2,1,0:T(8,128)}, u32[]{:S(2)}, u32[]{:S(2)}) async-start(f32[32,12,128]{2,1,0:T(8,128)} %maximum_bitcast_fusion), calls=%async_computation | async-start | bytes 524288 | tf_op jit(solution)/shard_map/all_to_all | solution.py:385
  60.0 3.4 %collective-permute-start = (f32[12,512]{1,0:T(8,128)}, f32[12,512]{1,0:T(8,128)}, u32[]{:S(2)}, u32[]{:S(2)}) collective-permute-start(f32[12,512]{1,0:T(8,128)} %copy-done.13), channel_id=1, source_target_pairs={{0,1},{1,2},{2,3},{3,4},{4,5},{5,6},{6,7},{7,8},{8,9},{9,10},{10,1... | collective-permute-start | bytes 73736 | tf_op jit(solution)/shard_map/ppermute | solution.py:33
  63.3 7.0 %collective-permute-start.1 = (f32[12,512]{1,0:T(8,128)}, f32[12,512]{1,0:T(8,128)}, u32[]{:S(2)}, u32[]{:S(2)}) collective-permute-start(f32[12,512]{1,0:T(8,128)} %copy-done.12), channel_id=1, source_target_pairs={{1,0},{2,1},{3,2},{4,3},{5,4},{6,5},{7,6},{8,7},{9,8},{10,9},{11,1... | collective-permute-start | bytes 73736 | tf_op jit(solution)/shard_map/ppermute | solution.py:33
  70.3 0.7 copy.44.refs_0_
  71.0 1.3 copy.45.refs_1_
  73.0 0.7 copy-done.7
  73.8 4.5 %place.7.refs_14_ = f32[12,16,512]{2,1,0:T(8,128)S(1)} custom-call(f32[32,12,128]{2,1,0:T(8,128)} %all-to-all-done.refs_0_, s32[32,128]{1,0:T(8,128)S(1)} %bitcast.14), custom_call_target="tpu_custom_call" | custom-call | tf_op jit(solution)/shard_map/place/pallas_call | solution.py:165
  78.3 4.5 %place.6.refs_14_ = f32[12,16,512]{2,1,0:T(8,128)S(1)} custom-call(f32[32,12,128]{2,1,0:T(8,128)} %all-to-all-done.refs_0_, s32[32,128]{1,0:T(8,128)S(1)} %bitcast.15), custom_call_target="tpu_custom_call" | custom-call | tf_op jit(solution)/shard_map/place/pallas_call | solution.py:165
  82.8 4.5 %place.5.refs_14_ = f32[12,16,512]{2,1,0:T(8,128)S(1)} custom-call(f32[32,12,128]{2,1,0:T(8,128)} %all-to-all-done.refs_0_, s32[32,128]{1,0:T(8,128)S(1)} %bitcast.16), custom_call_target="tpu_custom_call" | custom-call | tf_op jit(solution)/shard_map/place/pallas_call | solution.py:165
  87.3 4.5 %place.4.refs_14_ = f32[12,16,512]{2,1,0:T(8,128)S(1)} custom-call(f32[32,12,128]{2,1,0:T(8,128)} %all-to-all-done.refs_0_, s32[32,128]{1,0:T(8,128)S(1)} %bitcast.17), custom_call_target="tpu_custom_call" | custom-call | tf_op jit(solution)/shard_map/place/pallas_call | solution.py:165
  91.9 3.6 %sweep1.4 = (f32[2,6,64,512]{3,2,1,0:T(8,128)S(1)}, f32[2,6,16,512]{3,2,1,0:T(8,128)S(1)}, f32[12,512]{1,0:T(8,128)}, f32[12,512]{1,0:T(8,128)S(1)}) custom-call(f32[4,6,6]{2,1,0:T(8,128)S(1)} %copy.44.refs_0_, f32[2,6,6]{2,1,0:T(8,128)S(1)} %copy-done.6, f32[1]{0:T(128)S(6)} %copy.55.refs_2_, f32[2,6,64,512]{3,2,1,0:T(8,128)S(1)} %copy-done, ...), custom_call_target="tpu_custom_call" | custom-call | tf_op jit(solution)/shard_map/sweep1/pallas_call | solution.py:321
  95.5 3.7 %sweep1.5 = (f32[2,6,64,512]{3,2,1,0:T(8,128)S(1)}, f32[2,6,16,512]{3,2,1,0:T(8,128)S(1)}, f32[12,512]{1,0:T(8,128)}, f32[12,512]{1,0:T(8,128)}) custom-call(f32[4,6,6]{2,1,0:T(8,128)S(1)} %copy.44.refs_0_, f32[2,6,6]{2,1,0:T(8,128)S(1)} %copy-done.6, f32[1]{0:T(128)S(6)} %copy.55.refs_2_, ...), custom_call_target="tpu_custom_call", output_to_operand_aliasing={{0}: (18, {})} | custom-call | tf_op jit(solution)/shard_map/sweep1/pallas_call | solution.py:321
  99.2 0.7 collective-permute-start.16
  100.0 3.7 %sweep1.6 = (f32[2,6,64,512]{3,2,1,0:T(8,128)S(1)}, f32[2,6,16,512]{3,2,1,0:T(8,128)S(1)}, f32[12,512]{1,0:T(8,128)}, f32[12,512]{1,0:T(8,128)}) custom-call(f32[4,6,6]{2,1,0:T(8,128)S(1)} %copy.44.refs_0_, f32[2,6,6]{2,1,0:T(8,128)S(1)} %copy-done.6, f32[1]{0:T(128)S(6)} %copy.55.refs_2_, ...), custom_call_target="tpu_custom_call", output_to_operand_aliasing={{0}: (18, {})} | custom-call | tf_op jit(solution)/shard_map/sweep1/pallas_call | solution.py:321
  103.6 0.1 collective-permute-start.14
  103.8 3.7 %sweep1.7 = (f32[2,6,64,512]{3,2,1,0:T(8,128)S(1)}, f32[2,6,16,512]{3,2,1,0:T(8,128)S(1)}, f32[12,512]{1,0:T(8,128)S(1)}, f32[12,512]{1,0:T(8,128)}) custom-call(f32[4,6,6]{2,1,0:T(8,128)S(1)} %copy.44.refs_0_, f32[2,6,6]{2,1,0:T(8,128)S(1)} %copy-done.6, f32[1]{0:T(128)S(6)} %copy.55.refs_2_, ...), custom_call_target="tpu_custom_call", output_to_operand_aliasing={{0}: (18, {})} | custom-call | tf_op jit(solution)/shard_map/sweep1/pallas_call | solution.py:321
  107.5 0.4 collective-permute-start.12
  107.9 0.2 combine.7
  108.2 0.7 collective-permute-start.19
  108.8 0.2 combine.6
  109.1 1.5 collective-permute-start.17
  110.6 0.2 combine.5
  110.8 0.7 collective-permute-start.15
  111.5 0.2 combine.4
  111.7 1.5 collective-permute-start.13
  113.2 2.5 %collective-permute-start.11 = (f32[12,512]{1,0:T(8,128)S(1)}, f32[12,512]{1,0:T(8,128)S(1)}, u32[]{:S(2)}, u32[]{:S(2)}) collective-permute-start(f32[12,512]{1,0:T(8,128)S(1)} %get-tuple-element.29), channel_id=1, source_target_pairs={{1,0},{2,1},{3,2},{4,3},{5,4},{6,5},{7,6},{8,7},{9,8},{10,9},{11,1... | collective-permute-start | bytes 73736 | tf_op jit(solution)/shard_map/ppermute | solution.py:33
  115.7 27.7 %collective-permute-done.11.refs_7_ = f32[12,512]{1,0:T(8,128)S(1)} collective-permute-done((f32[12,512]{1,0:T(8,128)S(1)}, f32[12,512]{1,0:T(8,128)S(1)}, u32[]{:S(2)}, u32[]{:S(2)}) %collective-permute-start.11) | collective-permute-done | bytes 24608 | tf_op jit(solution)/shard_map/ppermute | solution.py:33
  143.5 1.9 %collective-permute-start.10 = (f32[12,512]{1,0:T(8,128)S(1)}, f32[12,512]{1,0:T(8,128)S(1)}, u32[]{:S(2)}, u32[]{:S(2)}) collective-permute-start(f32[12,512]{1,0:T(8,128)S(1)} %get-tuple-element.28), channel_id=1, source_target_pairs={{0,1},{1,2},{2,3},{3,4},{4,5},{5,6},{6,7},{7,8},{8,9},{9,10},{10,1... | collective-permute-start | bytes 73736 | tf_op jit(solution)/shard_map/ppermute | solution.py:33
  145.4 8.8 %collective-permute-done.10.refs_6_ = f32[12,512]{1,0:T(8,128)S(1)} collective-permute-done((f32[12,512]{1,0:T(8,128)S(1)}, f32[12,512]{1,0:T(8,128)S(1)}, u32[]{:S(2)}, u32[]{:S(2)}) %collective-permute-start.10) | collective-permute-done | bytes 24608 | tf_op jit(solution)/shard_map/ppermute | solution.py:33
  154.2 3.1 %sweep2.4 = (f32[2,6,64,512]{3,2,1,0:T(8,128)}, f32[2,6,64,512]{3,2,1,0:T(8,128)}) custom-call(f32[4,6,6]{2,1,0:T(8,128)S(1)} %copy.44.refs_0_, f32[2,6,6]{2,1,0:T(8,128)S(1)} %copy-done.6, f32[1]{0:T(128)S(6)} %copy.55.refs_2_, f32[2,6,64,512]{3,2,1,0:T(8,128)S(1)} %get-tuple-element.27.refs_3_.refs_4_.refs_5_, ...), custom_call_target="tpu_custom_call" | custom-call | tf_op jit(solution)/shard_map/sweep2/pallas_call | solution.py:321
  157.4 3.2 %sweep2.5 = (f32[2,6,64,512]{3,2,1,0:T(8,128)}, f32[2,6,64,512]{3,2,1,0:T(8,128)}) custom-call(f32[4,6,6]{2,1,0:T(8,128)S(1)} %copy.44.refs_0_, f32[2,6,6]{2,1,0:T(8,128)S(1)} %copy-done.6, f32[1]{0:T(128)S(6)} %copy.55.refs_2_, f32[2,6,64,512]{3,2,1,0:T(8,128)S(1)} %get-tuple-element.27.refs_3_.refs_4_.refs_5_, ...), custom_call_target="tpu_custom_call", output_to_operand_aliasing={{0}: (17, {}), {1}: (18, {})} | custom-call | tf_op jit(solution)/shard_map/sweep2/pallas_call | solution.py:321
  160.5 3.2 %sweep2.6 = (f32[2,6,64,512]{3,2,1,0:T(8,128)}, f32[2,6,64,512]{3,2,1,0:T(8,128)}) custom-call(f32[4,6,6]{2,1,0:T(8,128)S(1)} %copy.44.refs_0_, f32[2,6,6]{2,1,0:T(8,128)S(1)} %copy-done.6, f32[1]{0:T(128)S(6)} %copy.55.refs_2_, f32[2,6,64,512]{3,2,1,0:T(8,128)S(1)} %get-tuple-element.27.refs_3_.refs_4_.refs_5_, ...), custom_call_target="tpu_custom_call", output_to_operand_aliasing={{0}: (17, {}), {1}: (18, {})} | custom-call | tf_op jit(solution)/shard_map/sweep2/pallas_call | solution.py:321
  163.7 3.2 %sweep2.7 = (f32[2,6,64,512]{3,2,1,0:T(8,128)}, f32[2,6,64,512]{3,2,1,0:T(8,128)}) custom-call(f32[4,6,6]{2,1,0:T(8,128)S(1)} %copy.44.refs_0_, f32[2,6,6]{2,1,0:T(8,128)S(1)} %copy-done.6, f32[1]{0:T(128)S(6)} %copy.55.refs_2_, f32[2,6,64,512]{3,2,1,0:T(8,128)S(1)} %get-tuple-element.27.refs_3_.refs_4_.refs_5_, ...), custom_call_target="tpu_custom_call", output_to_operand_aliasing={{0}: (17, {}), {1}: (18, {})} | custom-call | tf_op jit(solution)/shard_map/sweep2/pallas_call | solution.py:321
  (47 shorter events, 0.1 us)
Async XLA Ops:
  0.6 3.1 %copy-start = (f32[2,6,64,512]{3,2,1,0:T(8,128)S(1)}, f32[2,6,64,512]{3,2,1,0:T(8,128)}, u32[]{:S(2)}) copy-start(f32[2,6,64,512]{3,2,1,0:T(8,128)} %refs_5_.7) | copy-start | bytes 4718596
  0.6 4.4 %copy-start.8 = (s32[1,32,128]{2,1,0:T(8,128)S(1)}, s32[1,32,128]{2,1,0:T(8,128)}, u32[]{:S(2)}) copy-start(s32[1,32,128]{2,1,0:T(8,128)} %param.26) | copy-start | bytes 49156
  0.7 4.4 %copy-start.9 = (f32[1,32,128]{2,1,0:T(8,128)S(1)}, f32[1,32,128]{2,1,0:T(8,128)}, u32[]{:S(2)}) copy-start(f32[1,32,128]{2,1,0:T(8,128)} %param.28) | copy-start | bytes 49156
  0.7 4.4 %copy-start.2 = (f32[2,64,512]{2,1,0:T(8,128)S(1)}, f32[2,64,512]{2,1,0:T(8,128)}, u32[]{:S(2)}) copy-start(f32[2,64,512]{2,1,0:T(8,128)} %refs_10_.15) | copy-start | bytes 786436
  0.7 4.4 %copy-start.10 = (f32[6,6]{1,0:T(8,128)S(1)}, f32[6,6]{1,0:T(8,128)}, u32[]{:S(2)}) copy-start(f32[6,6]{1,0:T(8,128)} %pb_ref.1) | copy-start | bytes 436
  0.7 4.4 %copy-start.11 = (s32[1,32]{1,0:T(1,128)S(1)}, s32[1,32]{1,0:T(1,128)}, u32[]{:S(2)}) copy-start(s32[1,32]{1,0:T(1,128)} %cnt_ref.1) | copy-start | bytes 388
  2.2 28.9 %collective-permute-start.6 = (f32[2,6,48,512]{3,2,1,0:T(8,128)S(1)}, f32[2,6,48,512]{3,2,1,0:T(8,128)S(1)}, u32[]{:S(2)}, u32[]{:S(2)}) collective-permute-start(f32[2,6,48,512]{3,2,1,0:T(8,128)S(1)} %slice.46), channel_id=1, source_target_pairs={{0,64},{32,96},{64,0},{96,32},{1,65},{33,97},{65,1},{97,33},{2,66}... | collective-permute-start | bytes 3538952 | tf_op jit(solution)/shard_map/ppermute | solution.py:27
  3.8 88.1 %collective-permute-start.5 = (f32[2,6,64,512]{3,2,1,0:T(8,128)S(1)}, f32[2,6,64,512]{3,2,1,0:T(8,128)}, u32[]{:S(2)}, u32[]{:S(2)}) collective-permute-start(f32[2,6,64,512]{3,2,1,0:T(8,128)S(1)} %copy-done), channel_id=1, source_target_pairs={{0,32},{32,0},{64,96},{96,64},{1,33},{33,1},{65,97},{97,65},{2,34}... | collective-permute-start | bytes 4718600 | tf_op jit(solution)/shard_map/ppermute | solution.py:27
  4.5 40.2 %collective-permute-start.8 = (f32[2,6,16,512]{3,2,1,0:T(8,128)}, f32[2,6,16,512]{3,2,1,0:T(8,128)}, u32[]{:S(2)}, u32[]{:S(2)}) collective-permute-start(f32[2,6,16,512]{3,2,1,0:T(8,128)} %slice.47), channel_id=1, source_target_pairs={{0,64},{32,96},{64,0},{96,32},{1,65},{33,97},{65,1},{97,33},{2,66}... | collective-permute-start | bytes 1179656 | tf_op jit(solution)/shard_map/ppermute | solution.py:27
  14.4 16.7 %copy-start.12 = (f32[12,512]{1,0:T(8,128)}, f32[12,512]{1,0:T(8,128)S(1)}, u32[]{:S(2)}) copy-start(f32[12,512]{1,0:T(8,128)S(1)} %get-tuple-element.22) | copy-start | bytes 73732
  14.4 16.7 %copy-start.13 = (f32[12,512]{1,0:T(8,128)}, f32[12,512]{1,0:T(8,128)S(1)}, u32[]{:S(2)}) copy-start(f32[12,512]{1,0:T(8,128)S(1)} %get-tuple-element.21) | copy-start | bytes 73732
  14.5 29.5 %collective-permute-start.2 = (f32[2,6,32,128]{3,1,2,0:T(8,128)S(1)}, f32[2,6,32,128]{3,1,2,0:T(8,128)S(1)}, u32[]{:S(2)}, u32[]{:S(2)}) collective-permute-start(f32[2,6,32,128]{3,1,2,0:T(8,128)S(1)} %copy.26), channel_id=1, source_target_pairs={{0,64},{32,96},{64,0},{96,32},{1,65},{33,97},{65,1},{97,33},{2,66}... | collective-permute-start | bytes 589832 | tf_op jit(solution)/shard_map/ppermute | solution.py:27
  31.1 64.4 %collective-permute-start.7 = (f32[2,6,48,512]{3,2,1,0:T(8,128)S(1)}, f32[2,6,48,512]{3,2,1,0:T(8,128)}, u32[]{:S(2)}, u32[]{:S(2)}) collective-permute-start(f32[2,6,48,512]{3,2,1,0:T(8,128)S(1)} %collective-permute-done.6.refs_16_), channel_id=1, source_target_pairs={{0,32},{32,0},{64,96},{96,64},{1,33},{33,1},{65,97},{97,65},{2,34}... | collective-permute-start | bytes 3538952 | tf_op jit(solution)/shard_map/ppermute | solution.py:27
  31.1 14.2 %collective-permute-start.4 = (f32[2,6,32,128]{3,1,2,0:T(8,128)S(1)}, f32[2,6,32,128]{3,1,2,0:T(8,128)}, u32[]{:S(2)}, u32[]{:S(2)}) collective-permute-start(f32[2,6,32,128]{3,1,2,0:T(8,128)S(1)} %copy.26), channel_id=1, source_target_pairs={{0,32},{32,0},{64,96},{96,64},{1,33},{33,1},{65,97},{97,65},{2,34}... | collective-permute-start | bytes 589832 | tf_op jit(solution)/shard_map/ppermute | solution.py:27
  44.0 1.7 collective-permute-start.3
  44.7 47.1 %collective-permute-start.9 = (f32[2,6,16,512]{3,2,1,0:T(8,128)}, f32[2,6,16,512]{3,2,1,0:T(8,128)}, u32[]{:S(2)}, u32[]{:S(2)}) collective-permute-start(f32[2,6,16,512]{3,2,1,0:T(8,128)} %collective-permute-done.8.refs_16_), channel_id=1, source_target_pairs={{0,32},{32,0},{64,96},{96,64},{1,33},{33,1},{65,97},{97,65},{2,34}... | collective-permute-start | bytes 1179656 | tf_op jit(solution)/shard_map/ppermute | solution.py:27
  48.7 43.1 %copy-start.3 = (f32[2,64,512]{2,1,0:T(8,128)S(1)}, f32[2,64,512]{2,1,0:T(8,128)}, u32[]{:S(2)}) copy-start(f32[2,64,512]{2,1,0:T(8,128)} %refs_11_.15) | copy-start | bytes 786436
  48.7 43.1 %copy-start.4 = (f32[2,64,512]{2,1,0:T(8,128)S(1)}, f32[2,64,512]{2,1,0:T(8,128)}, u32[]{:S(2)}) copy-start(f32[2,64,512]{2,1,0:T(8,128)} %refs_12_.15) | copy-start | bytes 786436
  48.7 24.2 %all-to-all-start = ((f32[32,12,128]{2,1,0:T(8,128)}), f32[32,12,128]{2,1,0:T(8,128)}, u32[]{:S(2)}, u32[]{:S(2)}) async-start(f32[32,12,128]{2,1,0:T(8,128)} %maximum_bitcast_fusion), calls=%async_computation | async-start | bytes 524288 | tf_op jit(solution)/shard_map/all_to_all | solution.py:385
  60.0 31.8 %collective-permute-start = (f32[12,512]{1,0:T(8,128)}, f32[12,512]{1,0:T(8,128)}, u32[]{:S(2)}, u32[]{:S(2)}) collective-permute-start(f32[12,512]{1,0:T(8,128)} %copy-done.13), channel_id=1, source_target_pairs={{0,1},{1,2},{2,3},{3,4},{4,5},{5,6},{6,7},{7,8},{8,9},{9,10},{10,1... | collective-permute-start | bytes 73736 | tf_op jit(solution)/shard_map/ppermute | solution.py:33
  63.3 28.5 %collective-permute-start.1 = (f32[12,512]{1,0:T(8,128)}, f32[12,512]{1,0:T(8,128)}, u32[]{:S(2)}, u32[]{:S(2)}) collective-permute-start(f32[12,512]{1,0:T(8,128)} %copy-done.12), channel_id=1, source_target_pairs={{1,0},{2,1},{3,2},{4,3},{5,4},{6,5},{7,6},{8,7},{9,8},{10,9},{11,1... | collective-permute-start | bytes 73736 | tf_op jit(solution)/shard_map/ppermute | solution.py:33
  73.0 18.9 %copy-start.5 = (f32[64,512]{1,0:T(8,128)S(1)}, f32[64,512]{1,0:T(8,128)}, u32[]{:S(2)}) copy-start(f32[64,512]{1,0:T(8,128)} %refs_13_.15) | copy-start | bytes 393220
  73.0 18.9 %copy-start.6 = (f32[2,6,6]{2,1,0:T(8,128)S(1)}, f32[2,6,6]{2,1,0:T(8,128)}, u32[]{:S(2)}) copy-start(f32[2,6,6]{2,1,0:T(8,128)} %copy.45.refs_1_) | copy-start | bytes 868
  73.0 0.8 copy-start.7
  95.5 12.4 %collective-permute-start.18 = (f32[2,6,16,512]{3,2,1,0:T(8,128)S(1)}, f32[2,6,16,512]{3,2,1,0:T(8,128)S(1)}, u32[]{:S(2)}, u32[]{:S(2)}) collective-permute-start(f32[2,6,16,512]{3,2,1,0:T(8,128)S(1)} %get-tuple-element.33.own), channel_id=1, source_target_pairs={{0,32},{32,0},{64,96},{96,64},{1,33},{33,1},{65,97},{97,65},{2,34}... | collective-permute-start | bytes 1179656 | tf_op jit(solution)/shard_map/ppermute | solution.py:27
  99.2 9.6 %collective-permute-start.16 = (f32[2,6,16,512]{3,2,1,0:T(8,128)S(1)}, f32[2,6,16,512]{3,2,1,0:T(8,128)S(1)}, u32[]{:S(2)}, u32[]{:S(2)}) collective-permute-start(f32[2,6,16,512]{3,2,1,0:T(8,128)S(1)} %get-tuple-element.32.own), channel_id=1, source_target_pairs={{0,32},{32,0},{64,96},{96,64},{1,33},{33,1},{65,97},{97,65},{2,34}... | collective-permute-start | bytes 1179656 | tf_op jit(solution)/shard_map/ppermute | solution.py:27
  103.6 7.0 %collective-permute-start.14 = (f32[2,6,16,512]{3,2,1,0:T(8,128)S(1)}, f32[2,6,16,512]{3,2,1,0:T(8,128)S(1)}, u32[]{:S(2)}, u32[]{:S(2)}) collective-permute-start(f32[2,6,16,512]{3,2,1,0:T(8,128)S(1)} %get-tuple-element.31.own), channel_id=1, source_target_pairs={{0,32},{32,0},{64,96},{96,64},{1,33},{33,1},{65,97},{97,65},{2,34}... | collective-permute-start | bytes 1179656 | tf_op jit(solution)/shard_map/ppermute | solution.py:27
  107.5 4.0 %collective-permute-start.12 = (f32[2,6,16,512]{3,2,1,0:T(8,128)S(1)}, f32[2,6,16,512]{3,2,1,0:T(8,128)S(1)}, u32[]{:S(2)}, u32[]{:S(2)}) collective-permute-start(f32[2,6,16,512]{3,2,1,0:T(8,128)S(1)} %get-tuple-element.30.own), channel_id=1, source_target_pairs={{0,32},{32,0},{64,96},{96,64},{1,33},{33,1},{65,97},{97,65},{2,34}... | collective-permute-start | bytes 1179656 | tf_op jit(solution)/shard_map/ppermute | solution.py:27
  108.2 46.1 %copy-start.1 = (f32[2,6,64,512]{3,2,1,0:T(8,128)S(1)}, f32[2,6,64,512]{3,2,1,0:T(8,128)}, u32[]{:S(2)}) copy-start(f32[2,6,64,512]{3,2,1,0:T(8,128)} %refs_8_.15) | copy-start | bytes 4718596
  108.2 37.2 %collective-permute-start.19 = (f32[2,6,16,512]{3,2,1,0:T(8,128)S(1)}, f32[2,6,16,512]{3,2,1,0:T(8,128)S(1)}, u32[]{:S(2)}, u32[]{:S(2)}) collective-permute-start(f32[2,6,16,512]{3,2,1,0:T(8,128)S(1)} %combine.7), channel_id=1, source_target_pairs={{0,64},{32,96},{64,0},{96,32},{1,65},{33,97},{65,1},{97,33},{2,66}... | collective-permute-start | bytes 1179656 | tf_op jit(solution)/shard_map/ppermute | solution.py:27
  109.1 48.3 %collective-permute-start.17 = (f32[2,6,16,512]{3,2,1,0:T(8,128)S(1)}, f32[2,6,16,512]{3,2,1,0:T(8,128)S(1)}, u32[]{:S(2)}, u32[]{:S(2)}) collective-permute-start(f32[2,6,16,512]{3,2,1,0:T(8,128)S(1)} %combine.6), channel_id=1, source_target_pairs={{0,64},{32,96},{64,0},{96,32},{1,65},{33,97},{65,1},{97,33},{2,66}... | collective-permute-start | bytes 1179656 | tf_op jit(solution)/shard_map/ppermute | solution.py:27
  110.8 49.7 %collective-permute-start.15 = (f32[2,6,16,512]{3,2,1,0:T(8,128)S(1)}, f32[2,6,16,512]{3,2,1,0:T(8,128)S(1)}, u32[]{:S(2)}, u32[]{:S(2)}) collective-permute-start(f32[2,6,16,512]{3,2,1,0:T(8,128)S(1)} %combine.5), channel_id=1, source_target_pairs={{0,64},{32,96},{64,0},{96,32},{1,65},{33,97},{65,1},{97,33},{2,66}... | collective-permute-start | bytes 1179656 | tf_op jit(solution)/shard_map/ppermute | solution.py:27
  111.7 51.9 %collective-permute-start.13 = (f32[2,6,16,512]{3,2,1,0:T(8,128)S(1)}, f32[2,6,16,512]{3,2,1,0:T(8,128)S(1)}, u32[]{:S(2)}, u32[]{:S(2)}) collective-permute-start(f32[2,6,16,512]{3,2,1,0:T(8,128)S(1)} %combine.4), channel_id=1, source_target_pairs={{0,64},{32,96},{64,0},{96,32},{1,65},{33,97},{65,1},{97,33},{2,66}... | collective-permute-start | bytes 1179656 | tf_op jit(solution)/shard_map/ppermute | solution.py:27
  113.2 30.2 %collective-permute-start.11 = (f32[12,512]{1,0:T(8,128)S(1)}, f32[12,512]{1,0:T(8,128)S(1)}, u32[]{:S(2)}, u32[]{:S(2)}) collective-permute-start(f32[12,512]{1,0:T(8,128)S(1)} %get-tuple-element.29), channel_id=1, source_target_pairs={{1,0},{2,1},{3,2},{4,3},{5,4},{6,5},{7,6},{8,7},{9,8},{10,9},{11,1... | collective-permute-start | bytes 73736 | tf_op jit(solution)/shard_map/ppermute | solution.py:33
  143.5 10.8 %collective-permute-start.10 = (f32[12,512]{1,0:T(8,128)S(1)}, f32[12,512]{1,0:T(8,128)S(1)}, u32[]{:S(2)}, u32[]{:S(2)}) collective-permute-start(f32[12,512]{1,0:T(8,128)S(1)} %get-tuple-element.28), channel_id=1, source_target_pairs={{0,1},{1,2},{2,3},{3,4},{4,5},{5,6},{6,7},{7,8},{8,9},{9,10},{10,1... | collective-permute-start | bytes 73736 | tf_op jit(solution)/shard_map/ppermute | solution.py:33
where the time goes:
time: 168 us; the launch traced here: 167 us
  waiting for transfers between devices  64.4 us (38%)
  Pallas kernels  55.5 us (33%)
  starting transfers between devices  36.4 us (22%)
  local copies, waits for them, and re-layouts  5.18 us (3%)
  other arithmetic  3.06 us (2%)
  between operations  2.35 us (1%)
    ppermute x4, waiting for transfers between devices, from_behind(): lax.ppermute(value, 'space', [(s, s + steps) for s in range(first, last)])  36.6 us
    ppermute x16, waiting for transfers between devices, partner(): return lax.ppermute(value, 'inst', [(i, i ^ bit) for i in range(4)])  27.8 us
    pallas_call x8, Pallas kernels, sweep(): pl.pallas_call(kernel, name='sweep2' if last_sweep else 'sweep1', grid=(n...  27.3 us
    pallas_call x4, Pallas kernels, place(): pl.pallas_call(kernel, name='place', grid=(4,), in_specs=[pl.BlockSpec((8...  18 us
    ppermute x4, starting transfers between devices, from_behind(): lax.ppermute(value, 'space', [(s, s + steps) for s in range(first, last)])  14.7 us
    all_to_all x1, starting transfers between devices, body(): lax.all_to_all(routed, 'space', split_axis=0, concat_axis=0, tiled=True)  11.2 us
    ppermute x16, starting transfers between devices, partner(): return lax.ppermute(value, 'inst', [(i, i ^ bit) for i in range(4)])  10.4 us
    pallas_call x1, Pallas kernels, pick(): pl.pallas_call(pick_kernel, name='pick', grid=(4,), in_specs=[smem(), sme...  9.29 us
  transfers between devices with their start and end apart: 21, of which 5 were waited for; matrix products, arithmetic and copies ran while one was open for 4% of the time, Pallas kernels for 31%

commit v1 on v0

v1 whole, which is shorter than its diff:
```python
import math

import jax
import jax.numpy as jnp
import numpy as np
from jax import lax
from jax.experimental import pallas as pl
from jax.experimental.pallas import tpu as pltpu
from jax.sharding import PartitionSpec as P

INSTANCES = 8
FIELDS = (0, 1, 2, 3, 4, 5, 8, 9, 10, 11, 12, 13)
BLK = 8
EDGE = (0, 2, 7)
PIECES = (EDGE, (1, 3, 1), (4, 3, 1))
VMEM = 40 * 1024 * 1024
MOST = 60 * 1024 * 1024
SMALL = pl.CostEstimate(flops=1024, transcendentals=0, bytes_accessed=4096)


def coef(k):
    k = k % INSTANCES
    if k in (0, 4):
        return 0.0
    return 0.5 * (-1.0) ** k / math.tan(math.pi * k / INSTANCES)


def partner(value, bit):
    return lax.ppermute(value, "inst", [(i, i ^ bit) for i in range(4)])


def halo_pairs(value, odd):
    count = lax.axis_size("space")
    pairs = [(p, p + 1) for p in range(odd, count - 1, 2)]
    return lax.ppermute(value, "space", pairs + [(q, p) for p, q in pairs])


def is_even():
    return lax.rem(lax.axis_index("space"), 2) == 0


def smem():
    return pl.BlockSpec(memory_space=pltpu.SMEM)


def params(limit=VMEM):
    return pltpu.CompilerParams(vmem_limit_bytes=limit)


def split(x):
    hi = x.astype(jnp.bfloat16)
    lo = (x - hi.astype(jnp.float32)).astype(jnp.bfloat16)
    return hi, lo


def pick_kernel(ndest, group, pb_ref, cnt_ref, a_ref, fs_ref, cell_ref, wt_ref, out_ref, lo_ref, hi_ref, tab):
    step = pl.program_id(0)
    even = is_even()

    @pl.when(step == 0)
    def _():
        for f in range(12):
            hi, lo = split(a_ref[f])
            tab[f * 64 : f * 64 + 64, 0:512] = hi
            tab[f * 64 : f * 64 + 64, 512:1024] = lo
        for f in range(12):
            last_row = fs_ref[f // 6, 7:8, :] * a_ref[f, 63:64, :]
            first_row = a_ref[f, 0:1, :]
            lo_ref[f : f + 1, :] = jnp.where(even, last_row, first_row)
            hi_ref[f : f + 1, :] = jnp.where(even, first_row, last_row)

    cells = cell_ref[...]
    cols = lax.bitwise_and(cells, 511)
    rows = lax.shift_right_logical(cells, 9)
    lane = lax.broadcasted_iota(jnp.int32, (512, 128), 0)
    sub = lax.broadcasted_iota(jnp.int32, (64, 128), 0)
    slot = lax.broadcasted_iota(jnp.int32, (1, 128), 1)
    for first in range(0, ndest, group):
        hot = jnp.concatenate(
            [
                jnp.where(lane == cols[q : q + 1, :], 1.0, 0.0).astype(jnp.bfloat16)
                for q in range(first, first + group)
            ],
            axis=1,
        )
        part = jnp.dot(tab[...], jnp.concatenate([hot, hot], axis=0), preferred_element_type=jnp.float32)
        for k in range(group):
            q = first + k
            mask = sub == rows[q : q + 1, :]
            weight = jnp.where(slot < cnt_ref[0, step * ndest + q], wt_ref[q : q + 1, :], 0.0)
            for g in range(2):
                got = []
                for v in range(6):
                    f = g * 6 + v
                    mine = part[f * 64 : f * 64 + 64, k * 128 : k * 128 + 128]
                    got.append(jnp.sum(jnp.where(mask, mine, 0.0), axis=0, keepdims=True))
                for u in range(6):
                    total = pb_ref[0, u] * got[0]
                    for v in range(1, 6):
                        total = total + pb_ref[v, u] * got[v]
                    out_ref[q, 8 * g + u : 8 * g + u + 1, :] = total * weight
                out_ref[q, 8 * g + 6 : 8 * g + 8, :] = jnp.zeros((2, 128), jnp.float32)


def pick(block, counts, a, fs, cells, weights, ndest=32, group=4):
    def kernel(*refs):
        pick_kernel(ndest, group, *refs)

    return pl.pallas_call(
        kernel,
        name="pick",
        grid=(32 // ndest,),
        in_specs=[
            smem(),
            smem(),
            pl.BlockSpec((12, 64, 512), lambda i: (0, 0, 0)),
            pl.BlockSpec((2, 8, 512), lambda i: (0, 7, 0)),
            pl.BlockSpec((ndest, 128), lambda i: (i, 0)),
            pl.BlockSpec((ndest, 128), lambda i: (i, 0)),
        ],
        out_specs=[
            pl.BlockSpec((ndest, 16, 128), lambda i: (i, 0, 0)),
            pl.BlockSpec((12, 512), lambda i: (0, 0)),
            pl.BlockSpec((12, 512), lambda i: (0, 0)),
        ],
        out_shape=[
            jax.ShapeDtypeStruct((32, 16, 128), jnp.float32),
            jax.ShapeDtypeStruct((12, 512), jnp.float32),
            jax.ShapeDtypeStruct((12, 512), jnp.float32),
        ],
        scratch_shapes=[pltpu.VMEM((768, 1024), jnp.bfloat16)],
        cost_estimate=SMALL,
        compiler_params=params(),
    )(block, counts, a, fs, cells, weights)


def pack_kernel(head, tail, out):
    out[:, :, 0:BLK, :] = head[...]
    out[:, :, BLK : 2 * BLK, :] = tail[...]


def pack(a):
    big = (2, 6, BLK, 512)
    return pl.pallas_call(
        pack_kernel,
        name="pack",
        grid=(1,),
        in_specs=[pl.BlockSpec(big, lambda i: (0, 0, 0, 0)), pl.BlockSpec(big, lambda i: (0, 0, 7, 0))],
        out_specs=pl.BlockSpec((2, 6, 2 * BLK, 512), lambda i: (0, 0, 0, 0)),
        out_shape=jax.ShapeDtypeStruct((2, 6, 2 * BLK, 512), jnp.float32),
        cost_estimate=SMALL,
        compiler_params=params(MOST),
    )(a, a)


def rows_of(a, piece):
    return a[:, :, piece[0] * BLK : (piece[0] + piece[1]) * BLK]


def route_kernel(shift_ref, own, sib, par, sp, out):
    position = lax.axis_index("inst")
    core = lax.rem(position, 2)
    chip = position - core
    sibling = chip + 1 - core
    far = 2 - chip
    homes = [position, sibling, far + core, far + 1 - core]
    for j in range(2):
        want = lax.rem(2 * position + j - shift_ref[0] + INSTANCES, INSTANCES)
        value = jnp.zeros((32, 8, 128), jnp.float32)
        for x, home in zip((own, sib, par, sp), homes):
            for i in range(2):
                value = jnp.where(want == 2 * home + i, x[:, 8 * i : 8 * i + 8, :], value)
        out[:, 8 * j : 8 * j + 8, :] = value


def route(shift, pieces):
    return pl.pallas_call(
        route_kernel,
        name="route",
        in_specs=[smem()] + [pl.BlockSpec(memory_space=pltpu.VMEM)] * 4,
        out_specs=pl.BlockSpec(memory_space=pltpu.VMEM),
        out_shape=jax.ShapeDtypeStruct((32, 16, 128), jnp.float32),
        cost_estimate=SMALL,
        compiler_params=params(),
    )(shift, *pieces)


def place_kernel(piece, ndest, val_ref, tgt_ref, out_ref):
    b0, nb, st = piece
    rows_here = nb * BLK
    step = pl.program_id(0)
    cells = tgt_ref[...]
    cols = lax.bitwise_and(cells, 511)
    rows = lax.shift_right_logical(cells, 9)
    if st == 1:
        rows = rows - b0 * BLK
    else:
        jump = (st - 1) * BLK
        rows = jnp.where(rows < BLK, rows, jnp.where(rows >= st * BLK, rows - jump, -1))
    lane = lax.broadcasted_iota(jnp.int32, (512, 128), 0)
    sub = lax.broadcasted_iota(jnp.int32, (rows_here, 128), 0)
    hot = jnp.concatenate(
        [jnp.where(lane == cols[p : p + 1, :], 1.0, 0.0).astype(jnp.bfloat16) for p in range(ndest)], axis=1
    )
    highs, lows = [], []
    for p in range(ndest):
        mask = sub == rows[p : p + 1, :]
        spread = [jnp.where(mask, val_ref[p, f : f + 1, :], 0.0) for f in FIELDS]
        hi, lo = split(jnp.concatenate(spread, axis=0))
        highs.append(hi)
        lows.append(lo)
    both = jnp.concatenate([jnp.concatenate(highs, axis=1), jnp.concatenate(lows, axis=1)], axis=0)
    total = lax.dot_general(both, hot, (((1,), (1,)), ((), ())), preferred_element_type=jnp.float32)
    total = (total[: 12 * rows_here] + total[12 * rows_here :]).reshape(12, rows_here, 512)
    if ndest == 32:
        out_ref[...] = total
        return

    @pl.when(step == 0)
    def _():
        out_ref[...] = total

    @pl.when(step > 0)
    def _():
        out_ref[...] += total


def place(values, targets, piece, ndest):
    rows = piece[1] * BLK

    def kernel(*refs):
        place_kernel(piece, ndest, *refs)

    return pl.pallas_call(
        kernel,
        name="place",
        grid=(32 // ndest,),
        in_specs=[
            pl.BlockSpec((ndest, 16, 128), lambda i: (i, 0, 0)),
            pl.BlockSpec((ndest, 128), lambda i: (i, 0)),
        ],
        out_specs=pl.BlockSpec((12, rows, 512), lambda i: (0, 0, 0)),
        out_shape=jax.ShapeDtypeStruct((12, rows, 512), jnp.float32),
        cost_estimate=SMALL,
        compiler_params=params(),
    )(values, targets)


def own_terms(core, j):
    own = [coef(i - j) for i in range(2)]
    sib = [(coef(2 + i - j), coef(-2 + i - j)) for i in range(2)]
    return own, [jnp.where(core == 0, jnp.float32(e), jnp.float32(o)) for e, o in sib]


def far_terms(core, j):
    par = [coef(4 + i - j) for i in range(2)]
    sp = [(coef(6 + i - j), coef(2 + i - j)) for i in range(2)]
    return par, [jnp.where(core == 0, jnp.float32(e), jnp.float32(o)) for e, o in sp]


def weighted(terms, fields):
    total = None
    for c, x in zip(terms, fields):
        if isinstance(c, float) and c == 0.0:
            continue
        total = c * x if total is None else total + c * x
    return total


def sweep_kernel(
    last_sweep, piece, nfar, cf_ref, fr_ref, cur, prev, nxt, hlo, hhi, src, fs_ref, fsp_ref, fp_ref, dg_ref,
    vol_ref, per_ref, sib, *rest,
):
    blk = piece[0] + piece[2] * pl.program_id(0)
    edge = piece == EDGE
    even = is_even()
    core = lax.rem(lax.axis_index("inst"), 2)
    far, rest = rest[:nfar], rest[nfar:]
    if last_sweep:
        out, res_out = rest[-2:]
    elif edge:
        out, copy, edge_lo, edge_hi = rest[-4:]
    else:
        out, copy = rest[-2:]
    row = lax.broadcasted_iota(jnp.int32, (BLK, 512), 0)
    col = lax.broadcasted_iota(jnp.int32, (BLK, 512), 1)
    top, bottom = row == 0, row == BLK - 1
    left, right = col == 0, col == 511
    fv = fr_ref[0] * vol_ref[...]
    for g in range(2):
        fs, fp, dg = fs_ref[g], fp_ref[g], dg_ref[g]
        fs_before = fsp_ref[g, BLK - 1 : BLK, :]
        own_w, sib_w = own_terms(core, g)
        if nfar == 2:
            par_w, sp_w = far_terms(core, g)
        r = [src[g, u] - per_ref[g * 6 + u] for u in range(6)]
        for v in range(6):
            f = g * 6 + v
            a = cur[g, v]
            before = fs_before * prev[g, v, BLK - 1 : BLK, :]
            after = nxt[g, v, 0:1, :]
            if edge:
                one, two = hlo[f : f + 1, :], hhi[f : f + 1, :]
                before = jnp.where(blk == 0, jnp.where(even, two, one), before)
                after = jnp.where(blk == 7, jnp.where(even, one, two), after)
            lower = jnp.where(top, before, pltpu.roll(fs * a, 1, 0))
            upper = fs * jnp.where(bottom, after, pltpu.roll(a, BLK - 1, 0))
            lft = jnp.where(left, 0.0, pltpu.roll(fp * a, 1, 1))
            rgt = fp * jnp.where(right, 0.0, pltpu.roll(a, 511, 1))
            for u in range(6):
                r[u] = r[u] - (
                    (cf_ref[0, v, u] * lower + cf_ref[1, v, u] * upper)
                    + (cf_ref[2, v, u] * lft + cf_ref[3, v, u] * rgt)
                )
            mixed = weighted(own_w + sib_w, [cur[0, v], cur[1, v], sib[0, v], sib[1, v]])
            if nfar == 2:
                par, sp = far
                mixed = mixed + weighted(par_w + sp_w, [par[0, v], par[1, v], sp[0, v], sp[1, v]])
            else:
                mixed = mixed + far[0][g, v]
            r[v] = r[v] - fv * mixed
        for u in range(6):
            total = cf_ref[4 + g, u, 0] * r[0]
            for v in range(1, 6):
                total = total + cf_ref[4 + g, u, v] * r[v]
            new = dg * total
            out[g, u] = new
            if last_sweep:
                res_out[g, u] = r[u]
            else:
                copy[g, u] = new
                if edge:
                    f = g * 6 + u

                    last_row = (fs * new)[BLK - 1 : BLK, :]
                    first_row = new[0:1, :]

                    @pl.when(jnp.logical_and(blk == 7, even))
                    def _(row=last_row, f=f):
                        edge_lo[f : f + 1, :] = row

                    @pl.when(jnp.logical_and(blk == 7, jnp.logical_not(even)))
                    def _(row=last_row, f=f):
                        edge_hi[f : f + 1, :] = row

                    @pl.when(jnp.logical_and(blk == 0, even))
                    def _(row=first_row, f=f):
                        edge_hi[f : f + 1, :] = row

                    @pl.when(jnp.logical_and(blk == 0, jnp.logical_not(even)))
                    def _(row=first_row, f=f):
                        edge_lo[f : f + 1, :] = row


def sweep(last_sweep, piece, common, a, halo, per, per_off, sib, sib_at, far, far_off, into):
    b0, nb, st = piece
    coefs, fr, src, fs, fp, dg, vol = common
    big = (2, 6, BLK, 512)
    small = (2, BLK, 512)

    def blk(i):
        return b0 + st * i

    def low(i):
        return jnp.maximum(blk(i) - 1, 0)

    def high(i):
        return jnp.minimum(blk(i) + 1, 7)

    def here(off):
        return pl.BlockSpec(big, lambda i: (0, 0, off + i, 0))

    whole = pl.BlockSpec(big, lambda i: (0, 0, blk(i), 0))
    halo_spec = pl.BlockSpec((12, 512), lambda i: (0, 0))
    specs = [
        smem(), smem(),
        whole,
        pl.BlockSpec(big, lambda i: (0, 0, low(i), 0)),
        pl.BlockSpec(big, lambda i: (0, 0, high(i), 0)),
        halo_spec, halo_spec,
        whole,
        pl.BlockSpec(small, lambda i: (0, blk(i), 0)),
        pl.BlockSpec(small, lambda i: (0, low(i), 0)),
        pl.BlockSpec(small, lambda i: (0, blk(i), 0)),
        pl.BlockSpec(small, lambda i: (0, blk(i), 0)),
        pl.BlockSpec((BLK, 512), lambda i: (blk(i), 0)),
        pl.BlockSpec((12, BLK, 512), lambda i: (0, per_off + i, 0)),
        whole if sib_at is None else here(sib_at),
    ]
    args = [coefs, fr, a, a, a, halo[0], halo[1], src, fs, fs, fp, dg, vol, per, sib]
    for x in far:
        specs.append(here(far_off))
        args.append(x)
    full = jax.ShapeDtypeStruct((2, 6, 64, 512), jnp.float32)
    out_specs, out_shape = [whole], [full]
    if last_sweep:
        out_specs.append(whole)
        out_shape.append(full)
    else:
        out_specs.append(here(0))
        out_shape.append(jax.ShapeDtypeStruct((2, 6, nb * BLK, 512), jnp.float32))
        if piece == EDGE:
            out_specs += [halo_spec, halo_spec]
            out_shape += [jax.ShapeDtypeStruct((12, 512), jnp.float32)] * 2
    aliases = {}
    for k, x in enumerate(into):
        aliases[len(args)] = k
        specs.append(pl.BlockSpec(memory_space=pl.ANY))
        args.append(x)

    def kernel(*refs):
        sweep_kernel(last_sweep, piece, len(far), *refs)

    return pl.pallas_call(
        kernel,
        name="sweep2" if last_sweep else "sweep1",
        grid=(nb,),
        in_specs=specs,
        out_specs=out_specs,
        out_shape=out_shape,
        input_output_aliases=aliases,
        cost_estimate=SMALL,
        compiler_params=params(),
    )(*args)


def body(
    adjoint_old, source_term, face_stream, face_pitch, diag_scale, volume, face_blocks, diag_inverse,
    periodic_block, frequency, phase_shift, periodic_cells, periodic_targets, periodic_weights, periodic_counts,
):
    barrier = lax.optimization_barrier

    first, second, third = PIECES

    edge_rows = pack(adjoint_old)
    par_first = partner(edge_rows, 2)
    early, _ = barrier((adjoint_old, edge_rows))
    rows2 = rows_of(early, second)
    par_second = partner(rows2, 2)
    early, _ = barrier((adjoint_old, rows2))
    out, lo, hi = pick(
        periodic_block, periodic_counts, early.reshape(12, 64, 512), face_stream, periodic_cells[0],
        periodic_weights[0],
    )
    out, par_first = barrier((out, par_first))
    arrived0 = lax.all_to_all(out, "space", split_axis=0, concat_axis=0, tiled=True)
    rows3, lo, hi, fb, di, _ = barrier((adjoint_old, lo, hi, face_blocks, diag_inverse, out))
    coefs = jnp.concatenate([fb, di], axis=0)
    halo0 = (halo_pairs(lo, 0), halo_pairs(hi, 1))
    rows3 = rows_of(rows3, third)
    arrived0, halo0, coefs = barrier((arrived0, halo0, coefs))
    common = (coefs, frequency, source_term, face_stream, face_pitch, diag_scale, volume)
    arrived_sib = partner(arrived0, 1)
    arrived_par = partner(arrived0, 2)
    rows3, arrived_par = barrier((rows3, arrived_par))
    par_third = partner(rows3, 2)
    arrived_sp = partner(arrived_par, 1)
    arrived = route(phase_shift, (arrived0, arrived_sib, arrived_par, arrived_sp))
    own, par_first, par_second, _ = barrier((adjoint_old, par_first, par_second, arrived0))
    sib0 = partner(own, 1)
    sp_first = partner(par_first, 1)
    sp_second = partner(par_second, 1)
    targets = periodic_targets[:, 0, :]

    per_first = place(arrived, targets, first, 32)
    a1, piece1, lo1, hi1 = sweep(
        False, first, common, adjoint_old, halo0, per_first, 0, sib0, None, (par_first, sp_first), 0, ()
    )
    par1_first = partner(piece1, 2)
    arrived2, _ = barrier((arrived, piece1))
    per_second = place(arrived2, targets, second, 32)
    a1, piece2 = sweep(
        False, second, common, adjoint_old, halo0, per_second, 0, sib0, None, (par_second, sp_second), 0, (a1,)
    )
    halo1 = (halo_pairs(lo1, 0), halo_pairs(hi1, 1))
    sent2, par1_first, halo1 = barrier((piece2, par1_first, halo1))
    par1_second = partner(sent2, 2)
    par_third, arrived3, _ = barrier((par_third, arrived, par1_first))
    sp_third = partner(par_third, 1)
    per_third = place(arrived3, targets, third, 16)
    a1, piece3 = sweep(
        False, third, common, adjoint_old, halo0, per_third, 0, sib0, None, (par_third, sp_third), 0, (a1,)
    )
    sent3, par1_second = barrier((piece3, par1_second))
    par1_third = partner(sent3, 2)
    piece1, piece2, _ = barrier((piece1, piece2, sent3))
    sib1_third = partner(piece3, 1)
    sib1_first = partner(piece1, 1)
    sib1_second = partner(piece2, 1)
    sp1_first = partner(par1_first, 1)
    sp1_second = partner(par1_second, 1)

    outs = sweep(True, second, common, a1, halo1, per_second, 0, sib1_second, 0, (par1_second, sp1_second), 0, ())
    outs = sweep(True, first, common, a1, halo1, per_first, 0, sib1_first, 0, (par1_first, sp1_first), 0, outs)
    par1_third, outs = barrier((par1_third, tuple(outs)))
    sp1_third = partner(par1_third, 1)
    outs = sweep(True, third, common, a1, halo1, per_third, 0, sib1_third, 0, (par1_third, sp1_third), 0, outs)
    return (outs[0], outs[1])


def solution(mesh):
    in_specs = (
        P("inst", None, "space", None),
        P("inst", None, "space", None),
        P("inst", "space", None),
        P("inst", "space", None),
        P("inst", "space", None),
        P("space", None),
        P(),
        P("inst", None, None),
        P(),
        P(),
        P(),
        P("space", None, None),
        P(None, "space", None),
        P("space", None, None),
        P("space", None),
    )
    out_specs = (P("inst", None, "space", None), P("inst", None, "space", None))
    return jax.shard_map(body, mesh=mesh, in_specs=in_specs, out_specs=out_specs, check_vma=False)
```

time: 168 us -> 115 us (0.68)
  waiting for transfers between devices: 64.4 us -> 34.6 us
  Pallas kernels: 55.5 us -> 41.1 us
  starting transfers between devices: 36.4 us -> 33 us
  local copies, waits for them, and re-layouts: 5.18 us -> 2.21 us
  other arithmetic: 3.06 us -> 0.62 us
    ppermute x4, waiting for transfers between devices: 36.6 us -> 8.64 us  [halo_pairs(): return lax.ppermute(value, 'space', pairs + [(q, p) for p, q in pairs])]
    pallas_call x9 -> x6, Pallas kernels: 28.2 us -> 19.4 us  [the longest x1 9.01 us: pick(): pl.pallas_call(kernel, name='pick', grid=(32 // ndest,), in_specs=[smem()...]
    pallas_call x8 -> x6, Pallas kernels: 27.3 us -> 21.7 us  [sweep(): pl.pallas_call(kernel, name='sweep2' if last_sweep else 'sweep1', grid=(n...]
    ppermute x16 -> x19, starting transfers between devices: 10.4 us -> 7.64 us  [partner(): return lax.ppermute(value, 'inst', [(i, i ^ bit) for i in range(4)])]
    select_n x2 -> x0, other arithmetic: 2.32 us -> none  [body(): value = jnp.where(want == 2 * home + i, x[i], value)]
    ppermute x16 -> x19, waiting for transfers between devices: 27.8 us -> 26 us  [partner(): return lax.ppermute(value, 'inst', [(i, i ^ bit) for i in range(4)])]
  transfers between devices with their start and end apart: 21 -> 24, of which waited for: 5 -> 9; matrix products, arithmetic and copies ran while one was open for 4% -> 1% of each run, Pallas kernels for 31% -> 31%
where the time goes in v1:
time: 115 us; the launch traced here: 114 us
  Pallas kernels  41.1 us (36%)
  waiting for transfers between devices  34.6 us (30%)
  starting transfers between devices  33 us (29%)
  between operations  2.31 us (2%)
  local copies, waits for them, and re-layouts  2.21 us (2%)
    ppermute x19, waiting for transfers between devices, partner(): return lax.ppermute(value, 'inst', [(i, i ^ bit) for i in range(4)])  26 us
    pallas_call x6, Pallas kernels, sweep(): pl.pallas_call(kernel, name='sweep2' if last_sweep else 'sweep1', grid=(n...  21.7 us
    ppermute x4, starting transfers between devices, halo_pairs(): return lax.ppermute(value, 'space', pairs + [(q, p) for p, q in pairs])  14.3 us
    all_to_all x1, starting transfers between devices, body(): lax.all_to_all(out, 'space', split_axis=0, concat_axis=0, tiled=True)  11.1 us
    pallas_call x1, Pallas kernels, pick(): pl.pallas_call(kernel, name='pick', grid=(32 // ndest,), in_specs=[smem()...  9.01 us
    ppermute x4, waiting for transfers between devices, halo_pairs(): return lax.ppermute(value, 'space', pairs + [(q, p) for p, q in pairs])  8.64 us
    ppermute x19, starting transfers between devices, partner(): return lax.ppermute(value, 'inst', [(i, i ^ bit) for i in range(4)])  7.64 us
    pallas_call x3, Pallas kernels, place(): pl.pallas_call(kernel, name='place', grid=(32 // ndest,), in_specs=[pl.Bl...  7.38 us
  transfers between devices with their start and end apart: 24, of which 9 were waited for; matrix products, arithmetic and copies ran while one was open for 1% of the time, Pallas kernels for 31%

profile of v1, /device:TPU:8, one launch (start us, length us, event | category | flops | bytes accessed | tf_op | source)
XLA Modules:
  0.0 113.8 jit_solution(5655388701039182089)
XLA Ops:
  0.7 1.9 %pack.1 = f32[2,6,16,512]{3,2,1,0:T(8,128)} custom-call(f32[2,6,64,512]{3,2,1,0:T(8,128)} %refs_4_.5, f32[2,6,64,512]{3,2,1,0:T(8,128)} %refs_4_.5), custom_call_target="tpu_custom_call" | custom-call | flops 1024 | bytes 4096 | tf_op jit(solution)/shard_map/pack/pallas_call | solution.py:144
  2.6 1.5 %collective-permute-start = (f32[2,6,16,512]{3,2,1,0:T(8,128)}, f32[2,6,16,512]{3,2,1,0:T(8,128)S(1)}, u32[]{:S(2)}, u32[]{:S(2)}) collective-permute-start(f32[2,6,16,512]{3,2,1,0:T(8,128)} %pack.1), channel_id=1, source_target_pairs={{0,64},{32,96},{64,0},{96,32},{1,65},{33,97},{65,1},{97,33},{2,66}... | collective-permute-start | bytes 1179656 | tf_op jit(solution)/shard_map/ppermute | solution.py:29
  4.1 0.9 slice.6
  5.0 0.5 collective-permute-start.7
  5.5 9.0 %pick.1 = (f32[32,16,128]{2,1,0:T(8,128)}, f32[12,512]{1,0:T(8,128)}, f32[12,512]{1,0:T(8,128)}) custom-call(f32[6,6]{1,0:T(8,128)S(1)} %copy-done.16, s32[1,32]{1,0:T(1,128)S(1)} %copy-done.17, f32[12,64,512]{2,1,0:T(8,128)S(1)} %bitcast.4, f32[2,64,512]{2,1,0:T(8,128)S(1)} %copy-done.2, s32[32,128]{1,0:T(8,128)S(1)} %bitcast.8, f32[32,128]{1,0:T(8,128)S(1)} %bitcast.9), custom_call_target="tpu_custom_call" | custom-call | flops 1024 | bytes 4096 | tf_op jit(solution)/shard_map/pick/pallas_call | solution.py:109
  14.5 0.3 collective-permute-done.refs_15_
  14.8 11.1 %all-to-all-start = ((f32[32,16,128]{2,1,0:T(8,128)}), f32[32,16,128]{2,1,0:T(8,128)}, u32[]{:S(2)}, u32[]{:S(2)}) async-start(f32[32,16,128]{2,1,0:T(8,128)} %get-tuple-element.52), calls=%async_computation | async-start | bytes 524288 | tf_op jit(solution)/shard_map/all_to_all | solution.py:446
  25.9 1.5 %collective-permute-start.1 = (f32[12,512]{1,0:T(8,128)}, f32[12,512]{1,0:T(8,128)S(1)}, u32[]{:S(2)}, u32[]{:S(2)}) collective-permute-start(f32[12,512]{1,0:T(8,128)} %get-tuple-element.55), channel_id=1, source_target_pairs={{0,1},{2,3},{4,5},{6,7},{8,9},{10,11},{12,13},{14,15},{16,17},{18,... | collective-permute-start | bytes 73736 | tf_op jit(solution)/shard_map/ppermute | solution.py:35
  27.5 6.4 %collective-permute-start.2 = (f32[12,512]{1,0:T(8,128)}, f32[12,512]{1,0:T(8,128)S(1)}, u32[]{:S(2)}, u32[]{:S(2)}) collective-permute-start(f32[12,512]{1,0:T(8,128)} %get-tuple-element.56), channel_id=1, source_target_pairs={{1,2},{3,4},{5,6},{7,8},{9,10},{11,12},{13,14},{15,16},{17,18},{19... | collective-permute-start | bytes 73736 | tf_op jit(solution)/shard_map/ppermute | solution.py:35
  33.9 0.6 pad_maximum_fusion.refs_0_
  34.5 0.6 copy-done.9
  35.1 2.9 %collective-permute-done.2.refs_6_ = f32[12,512]{1,0:T(8,128)S(1)} collective-permute-done((f32[12,512]{1,0:T(8,128)}, f32[12,512]{1,0:T(8,128)S(1)}, u32[]{:S(2)}, u32[]{:S(2)}) %collective-permute-start.2) | collective-permute-done | bytes 24608 | tf_op jit(solution)/shard_map/ppermute | solution.py:35
  38.0 0.6 copy-done.11
  38.6 0.0 all-to-all-done.own
  38.6 0.0 copy-start.8
  38.7 0.1 collective-permute-start.8
  38.8 0.7 collective-permute-start.3
  39.4 0.2 collective-permute-start.5
  39.6 0.4 collective-permute-start.9
  40.0 7.7 %collective-permute-done.3.par = f32[32,16,128]{2,1,0:T(8,128)S(1)} collective-permute-done((f32[32,16,128]{2,1,0:T(8,128)}, f32[32,16,128]{2,1,0:T(8,128)S(1)}, u32[]{:S(2)}, u32[]{:S(2)}) %collective-permute-start.3) | collective-permute-done | bytes 262176 | tf_op jit(solution)/shard_map/ppermute | solution.py:29
  47.7 0.0 collective-permute-start.6
  47.7 0.5 collective-permute-start.10
  48.2 0.6 collective-permute-start.4
  50.1 1.1 route.1.refs_0_
  51.2 1.8 %place.3.refs_13_ = f32[12,16,512]{2,1,0:T(8,128)S(1)} custom-call(f32[32,16,128]{2,1,0:T(8,128)S(1)} %route.1.refs_0_, s32[32,128]{1,0:T(8,128)S(1)} %bitcast.5), custom_call_target="tpu_custom_call" | custom-call | flops 1024 | bytes 4096 | tf_op jit(solution)/shard_map/place/pallas_call | solution.py:234
  53.0 0.0 collective-permute-done.8.refs_14_
  53.1 3.1 %sweep1.3 = (f32[2,6,64,512]{3,2,1,0:T(8,128)S(1)}, f32[2,6,16,512]{3,2,1,0:T(8,128)S(1)}, f32[12,512]{1,0:T(8,128)S(1)}, f32[12,512]{1,0:T(8,128)S(1)}) custom-call(f32[6,6,6]{2,1,0:T(8,128)S(1)} %copy-done.6, f32[1]{0:T(128)S(6)} %copy.31.refs_1_, f32[2,6,64,512]{3,2,1,0:T(8,128)S(1)} %copy-done, f32[2,6,64,512]{3,2,1,0:T(8,128)S(1)} %copy-done, ...), custom_call_target="tpu_custom_call" | custom-call | flops 1024 | bytes 4096 | tf_op jit(solution)/shard_map/sweep1/pallas_call | solution.py:414
  56.3 1.5 %collective-permute-start.11 = (f32[2,6,16,512]{3,2,1,0:T(8,128)S(1)}, f32[2,6,16,512]{3,2,1,0:T(8,128)S(1)}, u32[]{:S(2)}, u32[]{:S(2)}) collective-permute-start(f32[2,6,16,512]{3,2,1,0:T(8,128)S(1)} %get-tuple-element.86), channel_id=1, source_target_pairs={{0,64},{32,96},{64,0},{96,32},{1,65},{33,97},{65,1},{97,33},{2,66}... | collective-permute-start | bytes 1179656 | tf_op jit(solution)/shard_map/ppermute | solution.py:29
  57.8 6.4 %collective-permute-start.13 = (f32[12,512]{1,0:T(8,128)S(1)}, f32[12,512]{1,0:T(8,128)S(1)}, u32[]{:S(2)}, u32[]{:S(2)}) collective-permute-start(f32[12,512]{1,0:T(8,128)S(1)} %get-tuple-element.75), channel_id=1, source_target_pairs={{1,2},{3,4},{5,6},{7,8},{9,10},{11,12},{13,14},{15,16},{17,18},{19... | collective-permute-start | bytes 73736 | tf_op jit(solution)/shard_map/ppermute | solution.py:35
  64.2 2.6 %place.4.refs_13_ = f32[12,24,512]{2,1,0:T(8,128)S(1)} custom-call(f32[32,16,128]{2,1,0:T(8,128)S(1)} %route.1.refs_0_, s32[32,128]{1,0:T(8,128)S(1)} %bitcast.6), custom_call_target="tpu_custom_call" | custom-call | flops 1024 | bytes 4096 | tf_op jit(solution)/shard_map/place/pallas_call | solution.py:234
  66.8 0.0 collective-permute-done.10.refs_16_
  66.8 3.7 %sweep1.4 = (f32[2,6,64,512]{3,2,1,0:T(8,128)S(1)}, f32[2,6,24,512]{3,2,1,0:T(8,128)S(1)}) custom-call(f32[6,6,6]{2,1,0:T(8,128)S(1)} %copy-done.6, f32[1]{0:T(128)S(6)} %copy.31.refs_1_, f32[2,6,64,512]{3,2,1,0:T(8,128)S(1)} %copy-done, f32[2,6,64,512]{3,2,1,0:T(8,128)S(1)} %copy-done, ...), custom_call_target="tpu_custom_call", output_to_operand_aliasing={{0}: (17, {})} | custom-call | flops 1024 | bytes 4096 | tf_op jit(solution)/shard_map/sweep1/pallas_call | solution.py:414
  70.5 5.7 %collective-permute-done.13.refs_6_ = f32[12,512]{1,0:T(8,128)S(1)} collective-permute-done((f32[12,512]{1,0:T(8,128)S(1)}, f32[12,512]{1,0:T(8,128)S(1)}, u32[]{:S(2)}, u32[]{:S(2)}) %collective-permute-start.13) | collective-permute-done | bytes 24608 | tf_op jit(solution)/shard_map/ppermute | solution.py:35
  76.2 0.3 collective-permute-start.16
  76.5 2.9 %place.5.refs_13_ = f32[12,24,512]{2,1,0:T(8,128)S(1)} custom-call(f32[32,16,128]{2,1,0:T(8,128)S(1)} %route.1.refs_0_, s32[32,128]{1,0:T(8,128)S(1)} %bitcast.7), custom_call_target="tpu_custom_call" | custom-call | flops 1024 | bytes 4096 | tf_op jit(solution)/shard_map/place/pallas_call | solution.py:234
  79.5 3.5 %sweep1.5 = (f32[2,6,64,512]{3,2,1,0:T(8,128)S(1)}, f32[2,6,24,512]{3,2,1,0:T(8,128)S(1)}) custom-call(f32[6,6,6]{2,1,0:T(8,128)S(1)} %copy-done.6, f32[1]{0:T(128)S(6)} %copy.31.refs_1_, f32[2,6,64,512]{3,2,1,0:T(8,128)S(1)} %copy-done, f32[2,6,64,512]{3,2,1,0:T(8,128)S(1)} %copy-done, ...), custom_call_target="tpu_custom_call", output_to_operand_aliasing={{0}: (17, {})} | custom-call | flops 1024 | bytes 4096 | tf_op jit(solution)/shard_map/sweep1/pallas_call | solution.py:414
  83.0 9.0 %collective-permute-done.16.refs_15_ = f32[2,6,24,512]{3,2,1,0:T(8,128)S(1)} collective-permute-done((f32[2,6,24,512]{3,2,1,0:T(8,128)S(1)}, f32[2,6,24,512]{3,2,1,0:T(8,128)S(1)}, u32[]{:S(2)}, u32[]{:S(2)}) %collective-permute-start.16) | collective-permute-done | bytes 589856 | tf_op jit(solution)/shard_map/ppermute | solution.py:29
  92.0 0.5 collective-permute-start.21
  92.5 0.3 collective-permute-start.17
  92.8 0.5 collective-permute-start.18
  93.3 0.7 collective-permute-done.20.refs_14_
  94.0 0.1 collective-permute-start.15
  94.1 0.7 collective-permute-done.21.refs_16_
  94.8 4.1 %sweep2.3 = (f32[2,6,64,512]{3,2,1,0:T(8,128)}, f32[2,6,64,512]{3,2,1,0:T(8,128)}) custom-call(f32[6,6,6]{2,1,0:T(8,128)S(1)} %copy-done.6, f32[1]{0:T(128)S(6)} %copy.31.refs_1_, f32[2,6,64,512]{3,2,1,0:T(8,128)S(1)} %get-tuple-element.80.refs_2_.refs_3_.refs_4_, f32[2,6,64,512]{3,2,1,0:T(8,128)S(1)} %get-tuple-element.80.refs_2_.refs_3_.refs_4_, ...), custom_call_target="tpu_custom_call" | custom-call | flops 1024 | bytes 4096 | tf_op jit(solution)/shard_map/sweep2/pallas_call | solution.py:414
  98.9 3.3 %sweep2.4 = (f32[2,6,64,512]{3,2,1,0:T(8,128)}, f32[2,6,64,512]{3,2,1,0:T(8,128)}) custom-call(f32[6,6,6]{2,1,0:T(8,128)S(1)} %copy-done.6, f32[1]{0:T(128)S(6)} %copy.31.refs_1_, f32[2,6,64,512]{3,2,1,0:T(8,128)S(1)} %get-tuple-element.80.refs_2_.refs_3_.refs_4_, ...), custom_call_target="tpu_custom_call", output_to_operand_aliasing={{0}: (17, {}), {1}: (18, {})} | custom-call | flops 1024 | bytes 4096 | tf_op jit(solution)/shard_map/sweep2/pallas_call | solution.py:414
  102.2 5.5 %collective-permute-done.17.refs_15_ = f32[2,6,24,512]{3,2,1,0:T(8,128)S(1)} collective-permute-done((f32[2,6,24,512]{3,2,1,0:T(8,128)S(1)}, f32[2,6,24,512]{3,2,1,0:T(8,128)S(1)}, u32[]{:S(2)}, u32[]{:S(2)}) %collective-permute-start.17) | collective-permute-done | bytes 589856 | tf_op jit(solution)/shard_map/ppermute | solution.py:29
  107.7 2.0 %collective-permute-done.22.refs_16_ = f32[2,6,24,512]{3,2,1,0:T(8,128)S(1)} collective-permute-done((f32[2,6,24,512]{3,2,1,0:T(8,128)S(1)}, f32[2,6,24,512]{3,2,1,0:T(8,128)S(1)}, u32[]{:S(2)}, u32[]{:S(2)}) %collective-permute-start.22) | collective-permute-done | bytes 589856 | tf_op jit(solution)/shard_map/ppermute | solution.py:29
  109.7 4.1 %sweep2.5 = (f32[2,6,64,512]{3,2,1,0:T(8,128)}, f32[2,6,64,512]{3,2,1,0:T(8,128)}) custom-call(f32[6,6,6]{2,1,0:T(8,128)S(1)} %copy-done.6, f32[1]{0:T(128)S(6)} %copy.31.refs_1_, f32[2,6,64,512]{3,2,1,0:T(8,128)S(1)} %get-tuple-element.80.refs_2_.refs_3_.refs_4_, ...), custom_call_target="tpu_custom_call", output_to_operand_aliasing={{0}: (17, {}), {1}: (18, {})} | custom-call | flops 1024 | bytes 4096 | tf_op jit(solution)/shard_map/sweep2/pallas_call | solution.py:414
  (57 shorter events, 0.2 us)
Async XLA Ops:
  0.6 3.5 %copy-start = (f32[2,6,64,512]{3,2,1,0:T(8,128)S(1)}, f32[2,6,64,512]{3,2,1,0:T(8,128)}, u32[]{:S(2)}) copy-start(f32[2,6,64,512]{3,2,1,0:T(8,128)} %refs_4_.5) | copy-start | bytes 4718596
  0.6 4.9 %copy-start.14 = (s32[1,32,128]{2,1,0:T(8,128)S(1)}, s32[1,32,128]{2,1,0:T(8,128)}, u32[]{:S(2)}) copy-start(s32[1,32,128]{2,1,0:T(8,128)} %param.26) | copy-start | bytes 49156
  0.7 4.9 %copy-start.15 = (f32[1,32,128]{2,1,0:T(8,128)S(1)}, f32[1,32,128]{2,1,0:T(8,128)}, u32[]{:S(2)}) copy-start(f32[1,32,128]{2,1,0:T(8,128)} %param.28) | copy-start | bytes 49156
  0.7 4.9 %copy-start.2 = (f32[2,64,512]{2,1,0:T(8,128)S(1)}, f32[2,64,512]{2,1,0:T(8,128)}, u32[]{:S(2)}) copy-start(f32[2,64,512]{2,1,0:T(8,128)} %refs_9_.11) | copy-start | bytes 786436
  0.7 4.8 %copy-start.16 = (f32[6,6]{1,0:T(8,128)S(1)}, f32[6,6]{1,0:T(8,128)}, u32[]{:S(2)}) copy-start(f32[6,6]{1,0:T(8,128)} %refs_0_.1) | copy-start | bytes 436
  0.7 4.8 %copy-start.17 = (s32[1,32]{1,0:T(1,128)S(1)}, s32[1,32]{1,0:T(1,128)}, u32[]{:S(2)}) copy-start(s32[1,32]{1,0:T(1,128)} %refs_1_.7) | copy-start | bytes 388
  2.6 23.3 %copy-start.18 = (f32[4,6,6]{2,0,1:T(4,128)S(1)}, f32[4,6,6]{2,0,1:T(4,128)}, u32[]{:S(2)}) copy-start(f32[4,6,6]{2,0,1:T(4,128)} %param.21) | copy-start | bytes 1732
  2.6 23.3 %copy-start.19 = (f32[2,6,6]{2,0,1:T(2,128)S(1)}, f32[2,6,6]{2,0,1:T(2,128)}, u32[]{:S(2)}) copy-start(f32[2,6,6]{2,0,1:T(2,128)} %param.22) | copy-start | bytes 868
  2.6 12.2 %collective-permute-start = (f32[2,6,16,512]{3,2,1,0:T(8,128)}, f32[2,6,16,512]{3,2,1,0:T(8,128)S(1)}, u32[]{:S(2)}, u32[]{:S(2)}) collective-permute-start(f32[2,6,16,512]{3,2,1,0:T(8,128)} %pack.1), channel_id=1, source_target_pairs={{0,64},{32,96},{64,0},{96,32},{1,65},{33,97},{65,1},{97,33},{2,66}... | collective-permute-start | bytes 1179656 | tf_op jit(solution)/shard_map/ppermute | solution.py:29
  5.0 33.7 %collective-permute-start.7 = (f32[2,6,24,512]{3,2,1,0:T(8,128)}, f32[2,6,24,512]{3,2,1,0:T(8,128)}, u32[]{:S(2)}, u32[]{:S(2)}) collective-permute-start(f32[2,6,24,512]{3,2,1,0:T(8,128)} %slice.6), channel_id=1, source_target_pairs={{0,64},{32,96},{64,0},{96,32},{1,65},{33,97},{65,1},{97,33},{2,66}... | collective-permute-start | bytes 1769480 | tf_op jit(solution)/shard_map/ppermute | solution.py:29
  14.5 36.7 %copy-start.13 = (s32[32,1,128]{2,1,0:T(1,128)S(1)}, s32[32,1,128]{2,1,0:T(1,128)}, u32[]{:S(2)}) copy-start(s32[32,1,128]{2,1,0:T(1,128)} %param.27) | copy-start | bytes 49156
  14.8 19.0 %copy-start.7 = (f32[2,6,16,512]{3,2,1,0:T(8,128)}, f32[2,6,16,512]{3,2,1,0:T(8,128)S(1)}, u32[]{:S(2)}) copy-start(f32[2,6,16,512]{3,2,1,0:T(8,128)S(1)} %collective-permute-done.refs_15_) | copy-start | bytes 1179652
  14.8 23.8 %all-to-all-start = ((f32[32,16,128]{2,1,0:T(8,128)}), f32[32,16,128]{2,1,0:T(8,128)}, u32[]{:S(2)}, u32[]{:S(2)}) async-start(f32[32,16,128]{2,1,0:T(8,128)} %get-tuple-element.52), calls=%async_computation | async-start | bytes 524288 | tf_op jit(solution)/shard_map/all_to_all | solution.py:446
  25.9 8.6 %collective-permute-start.1 = (f32[12,512]{1,0:T(8,128)}, f32[12,512]{1,0:T(8,128)S(1)}, u32[]{:S(2)}, u32[]{:S(2)}) collective-permute-start(f32[12,512]{1,0:T(8,128)} %get-tuple-element.55), channel_id=1, source_target_pairs={{0,1},{2,3},{4,5},{6,7},{8,9},{10,11},{12,13},{14,15},{16,17},{18,... | collective-permute-start | bytes 73736 | tf_op jit(solution)/shard_map/ppermute | solution.py:35
  27.5 10.5 %collective-permute-start.2 = (f32[12,512]{1,0:T(8,128)}, f32[12,512]{1,0:T(8,128)S(1)}, u32[]{:S(2)}, u32[]{:S(2)}) collective-permute-start(f32[12,512]{1,0:T(8,128)} %get-tuple-element.56), channel_id=1, source_target_pairs={{1,2},{3,4},{5,6},{7,8},{9,10},{11,12},{13,14},{15,16},{17,18},{19... | collective-permute-start | bytes 73736 | tf_op jit(solution)/shard_map/ppermute | solution.py:35
  34.5 18.6 %copy-start.1 = (f32[2,6,64,512]{3,2,1,0:T(8,128)S(1)}, f32[2,6,64,512]{3,2,1,0:T(8,128)}, u32[]{:S(2)}) copy-start(f32[2,6,64,512]{3,2,1,0:T(8,128)} %refs_7_.11) | copy-start | bytes 4718596
  34.5 18.6 %copy-start.5 = (f32[64,512]{1,0:T(8,128)S(1)}, f32[64,512]{1,0:T(8,128)}, u32[]{:S(2)}) copy-start(f32[64,512]{1,0:T(8,128)} %refs_12_.11) | copy-start | bytes 393220
  34.5 0.6 copy-start.9
  38.0 0.6 copy-start.11
  38.6 14.5 %copy-start.3 = (f32[2,64,512]{2,1,0:T(8,128)S(1)}, f32[2,64,512]{2,1,0:T(8,128)}, u32[]{:S(2)}) copy-start(f32[2,64,512]{2,1,0:T(8,128)} %refs_10_.11) | copy-start | bytes 786436
  38.6 14.5 %copy-start.4 = (f32[2,64,512]{2,1,0:T(8,128)S(1)}, f32[2,64,512]{2,1,0:T(8,128)}, u32[]{:S(2)}) copy-start(f32[2,64,512]{2,1,0:T(8,128)} %refs_11_.11) | copy-start | bytes 786436
  38.6 14.5 %copy-start.6 = (f32[6,6,6]{2,1,0:T(8,128)S(1)}, f32[6,6,6]{2,1,0:T(8,128)}, u32[]{:S(2)}) copy-start(f32[6,6,6]{2,1,0:T(8,128)} %pad_maximum_fusion.refs_0_) | copy-start | bytes 2596
  38.6 14.5 %copy-start.8 = (f32[2,6,16,512]{3,2,1,0:T(8,128)S(1)}, f32[2,6,16,512]{3,2,1,0:T(8,128)}, u32[]{:S(2)}) copy-start(f32[2,6,16,512]{3,2,1,0:T(8,128)} %copy-done.7) | copy-start | bytes 1179652
  38.6 14.5 %copy-start.10 = (f32[12,512]{1,0:T(8,128)S(1)}, f32[12,512]{1,0:T(8,128)}, u32[]{:S(2)}) copy-start(f32[12,512]{1,0:T(8,128)} %copy-done.9) | copy-start | bytes 73732
  38.7 14.5 %copy-start.12 = (f32[12,512]{1,0:T(8,128)S(1)}, f32[12,512]{1,0:T(8,128)}, u32[]{:S(2)}) copy-start(f32[12,512]{1,0:T(8,128)} %copy-done.11) | copy-start | bytes 73732
  38.7 14.4 %collective-permute-start.8 = (f32[2,6,64,512]{3,2,1,0:T(8,128)S(1)}, f32[2,6,64,512]{3,2,1,0:T(8,128)S(1)}, u32[]{:S(2)}, u32[]{:S(2)}) collective-permute-start(f32[2,6,64,512]{3,2,1,0:T(8,128)S(1)} %copy-done), channel_id=1, source_target_pairs={{0,32},{32,0},{64,96},{96,64},{1,33},{33,1},{65,97},{97,65},{2,34}... | collective-permute-start | bytes 4718600 | tf_op jit(solution)/shard_map/ppermute | solution.py:29
  38.8 8.9 %collective-permute-start.3 = (f32[32,16,128]{2,1,0:T(8,128)}, f32[32,16,128]{2,1,0:T(8,128)S(1)}, u32[]{:S(2)}, u32[]{:S(2)}) collective-permute-start(f32[32,16,128]{2,1,0:T(8,128)} %all-to-all-done.own), channel_id=1, source_target_pairs={{0,64},{32,96},{64,0},{96,32},{1,65},{33,97},{65,1},{97,33},{2,66}... | collective-permute-start | bytes 786440 | tf_op jit(solution)/shard_map/ppermute | solution.py:29
  39.4 8.8 %collective-permute-start.5 = (f32[32,16,128]{2,1,0:T(8,128)}, f32[32,16,128]{2,1,0:T(8,128)S(1)}, u32[]{:S(2)}, u32[]{:S(2)}) collective-permute-start(f32[32,16,128]{2,1,0:T(8,128)} %all-to-all-done.own), channel_id=1, source_target_pairs={{0,32},{32,0},{64,96},{96,64},{1,33},{33,1},{65,97},{97,65},{2,34}... | collective-permute-start | bytes 786440 | tf_op jit(solution)/shard_map/ppermute | solution.py:29
  39.6 13.4 %collective-permute-start.9 = (f32[2,6,16,512]{3,2,1,0:T(8,128)}, f32[2,6,16,512]{3,2,1,0:T(8,128)S(1)}, u32[]{:S(2)}, u32[]{:S(2)}) collective-permute-start(f32[2,6,16,512]{3,2,1,0:T(8,128)} %copy-done.7), channel_id=1, source_target_pairs={{0,32},{32,0},{64,96},{96,64},{1,33},{33,1},{65,97},{97,65},{2,34}... | collective-permute-start | bytes 1179656 | tf_op jit(solution)/shard_map/ppermute | solution.py:29
  47.7 2.4 %collective-permute-start.6 = (f32[32,16,128]{2,1,0:T(8,128)S(1)}, f32[32,16,128]{2,1,0:T(8,128)S(1)}, u32[]{:S(2)}, u32[]{:S(2)}) collective-permute-start(f32[32,16,128]{2,1,0:T(8,128)S(1)} %collective-permute-done.3.par), channel_id=1, source_target_pairs={{0,32},{32,0},{64,96},{96,64},{1,33},{33,1},{65,97},{97,65},{2,34}... | collective-permute-start | bytes 786440 | tf_op jit(solution)/shard_map/ppermute | solution.py:29
  47.7 19.1 %collective-permute-start.10 = (f32[2,6,24,512]{3,2,1,0:T(8,128)}, f32[2,6,24,512]{3,2,1,0:T(8,128)S(1)}, u32[]{:S(2)}, u32[]{:S(2)}) collective-permute-start(f32[2,6,24,512]{3,2,1,0:T(8,128)} %collective-permute-done.7.refs_15_), channel_id=1, source_target_pairs={{0,32},{32,0},{64,96},{96,64},{1,33},{33,1},{65,97},{97,65},{2,34}... | collective-permute-start | bytes 1769480 | tf_op jit(solution)/shard_map/ppermute | solution.py:29
  48.2 28.0 %collective-permute-start.4 = (f32[2,6,24,512]{3,2,1,0:T(8,128)S(1)}, f32[2,6,24,512]{3,2,1,0:T(8,128)S(1)}, u32[]{:S(2)}, u32[]{:S(2)}) collective-permute-start(f32[2,6,24,512]{3,2,1,0:T(8,128)S(1)} %slice.7), channel_id=1, source_target_pairs={{0,64},{32,96},{64,0},{96,32},{1,65},{33,97},{65,1},{97,33},{2,66}... | collective-permute-start | bytes 1769480 | tf_op jit(solution)/shard_map/ppermute | solution.py:29
  56.3 19.9 %collective-permute-start.11 = (f32[2,6,16,512]{3,2,1,0:T(8,128)S(1)}, f32[2,6,16,512]{3,2,1,0:T(8,128)S(1)}, u32[]{:S(2)}, u32[]{:S(2)}) collective-permute-start(f32[2,6,16,512]{3,2,1,0:T(8,128)S(1)} %get-tuple-element.86), channel_id=1, source_target_pairs={{0,64},{32,96},{64,0},{96,32},{1,65},{33,97},{65,1},{97,33},{2,66}... | collective-permute-start | bytes 1179656 | tf_op jit(solution)/shard_map/ppermute | solution.py:29
  57.8 12.7 %collective-permute-start.12 = (f32[12,512]{1,0:T(8,128)S(1)}, f32[12,512]{1,0:T(8,128)S(1)}, u32[]{:S(2)}, u32[]{:S(2)}) collective-permute-start(f32[12,512]{1,0:T(8,128)S(1)} %get-tuple-element.74), channel_id=1, source_target_pairs={{0,1},{2,3},{4,5},{6,7},{8,9},{10,11},{12,13},{14,15},{16,17},{18,... | collective-permute-start | bytes 73736 | tf_op jit(solution)/shard_map/ppermute | solution.py:35
  57.8 18.4 %collective-permute-start.13 = (f32[12,512]{1,0:T(8,128)S(1)}, f32[12,512]{1,0:T(8,128)S(1)}, u32[]{:S(2)}, u32[]{:S(2)}) collective-permute-start(f32[12,512]{1,0:T(8,128)S(1)} %get-tuple-element.75), channel_id=1, source_target_pairs={{1,2},{3,4},{5,6},{7,8},{9,10},{11,12},{13,14},{15,16},{17,18},{19... | collective-permute-start | bytes 73736 | tf_op jit(solution)/shard_map/ppermute | solution.py:35
  76.2 3.3 %collective-permute-start.14 = (f32[2,6,24,512]{3,2,1,0:T(8,128)S(1)}, f32[2,6,24,512]{3,2,1,0:T(8,128)S(1)}, u32[]{:S(2)}, u32[]{:S(2)}) collective-permute-start(f32[2,6,24,512]{3,2,1,0:T(8,128)S(1)} %collective-permute-done.4.refs_15_), channel_id=1, source_target_pairs={{0,32},{32,0},{64,96},{96,64},{1,33},{33,1},{65,97},{97,65},{2,34}... | collective-permute-start | bytes 1769480 | tf_op jit(solution)/shard_map/ppermute | solution.py:29
  76.2 15.8 %collective-permute-start.16 = (f32[2,6,24,512]{3,2,1,0:T(8,128)S(1)}, f32[2,6,24,512]{3,2,1,0:T(8,128)S(1)}, u32[]{:S(2)}, u32[]{:S(2)}) collective-permute-start(f32[2,6,24,512]{3,2,1,0:T(8,128)S(1)} %get-tuple-element.87), channel_id=1, source_target_pairs={{0,64},{32,96},{64,0},{96,32},{1,65},{33,97},{65,1},{97,33},{2,66}... | collective-permute-start | bytes 1769480 | tf_op jit(solution)/shard_map/ppermute | solution.py:29
  92.0 2.0 %collective-permute-start.20 = (f32[2,6,24,512]{3,2,1,0:T(8,128)S(1)}, f32[2,6,24,512]{3,2,1,0:T(8,128)S(1)}, u32[]{:S(2)}, u32[]{:S(2)}) collective-permute-start(f32[2,6,24,512]{3,2,1,0:T(8,128)S(1)} %get-tuple-element.87), channel_id=1, source_target_pairs={{0,32},{32,0},{64,96},{96,64},{1,33},{33,1},{65,97},{97,65},{2,34}... | collective-permute-start | bytes 1769480 | tf_op jit(solution)/shard_map/ppermute | solution.py:29
  92.0 2.8 %collective-permute-start.21 = (f32[2,6,24,512]{3,2,1,0:T(8,128)S(1)}, f32[2,6,24,512]{3,2,1,0:T(8,128)S(1)}, u32[]{:S(2)}, u32[]{:S(2)}) collective-permute-start(f32[2,6,24,512]{3,2,1,0:T(8,128)S(1)} %collective-permute-done.16.refs_15_), channel_id=1, source_target_pairs={{0,32},{32,0},{64,96},{96,64},{1,33},{33,1},{65,97},{97,65},{2,34}... | collective-permute-start | bytes 1769480 | tf_op jit(solution)/shard_map/ppermute | solution.py:29
  92.5 15.2 %collective-permute-start.17 = (f32[2,6,24,512]{3,2,1,0:T(8,128)S(1)}, f32[2,6,24,512]{3,2,1,0:T(8,128)S(1)}, u32[]{:S(2)}, u32[]{:S(2)}) collective-permute-start(f32[2,6,24,512]{3,2,1,0:T(8,128)S(1)} %get-tuple-element.85), channel_id=1, source_target_pairs={{0,64},{32,96},{64,0},{96,32},{1,65},{33,97},{65,1},{97,33},{2,66}... | collective-permute-start | bytes 1769480 | tf_op jit(solution)/shard_map/ppermute | solution.py:29
  92.8 6.1 %collective-permute-start.19 = (f32[2,6,16,512]{3,2,1,0:T(8,128)S(1)}, f32[2,6,16,512]{3,2,1,0:T(8,128)S(1)}, u32[]{:S(2)}, u32[]{:S(2)}) collective-permute-start(f32[2,6,16,512]{3,2,1,0:T(8,128)S(1)} %collective-permute-done.11.refs_15_), channel_id=1, source_target_pairs={{0,32},{32,0},{64,96},{96,64},{1,33},{33,1},{65,97},{97,65},{2,34}... | collective-permute-start | bytes 1179656 | tf_op jit(solution)/shard_map/ppermute | solution.py:29
  92.8 6.1 %collective-permute-start.18 = (f32[2,6,16,512]{3,2,1,0:T(8,128)S(1)}, f32[2,6,16,512]{3,2,1,0:T(8,128)S(1)}, u32[]{:S(2)}, u32[]{:S(2)}) collective-permute-start(f32[2,6,16,512]{3,2,1,0:T(8,128)S(1)} %get-tuple-element.86), channel_id=1, source_target_pairs={{0,32},{32,0},{64,96},{96,64},{1,33},{33,1},{65,97},{97,65},{2,34}... | collective-permute-start | bytes 1179656 | tf_op jit(solution)/shard_map/ppermute | solution.py:29
  94.0 13.7 %collective-permute-start.15 = (f32[2,6,24,512]{3,2,1,0:T(8,128)S(1)}, f32[2,6,24,512]{3,2,1,0:T(8,128)S(1)}, u32[]{:S(2)}, u32[]{:S(2)}) collective-permute-start(f32[2,6,24,512]{3,2,1,0:T(8,128)S(1)} %get-tuple-element.85), channel_id=1, source_target_pairs={{0,32},{32,0},{64,96},{96,64},{1,33},{33,1},{65,97},{97,65},{2,34}... | collective-permute-start | bytes 1769480 | tf_op jit(solution)/shard_map/ppermute | solution.py:29
  107.7 2.0 %collective-permute-start.22 = (f32[2,6,24,512]{3,2,1,0:T(8,128)S(1)}, f32[2,6,24,512]{3,2,1,0:T(8,128)S(1)}, u32[]{:S(2)}, u32[]{:S(2)}) collective-permute-start(f32[2,6,24,512]{3,2,1,0:T(8,128)S(1)} %collective-permute-done.17.refs_15_), channel_id=1, source_target_pairs={{0,32},{32,0},{64,96},{96,64},{1,33},{33,1},{65,97},{97,65},{2,34}... | collective-permute-start | bytes 1769480 | tf_op jit(solution)/shard_map/ppermute | solution.py:29
